TPU v7x, 32 devices: a whole 2x2x4 slice. The times are simulated.
32 devices in a mesh: row: 8 (over z, core), col: 4 (over y, x).
Axes of the slice: x: 2, y: 2, z: 4, core: 2. Of those that a mesh axis runs over, the one named last changes fastest.
Arguments:
- ancestor: float32 [8, 1536, 12288], P(None, 'col', 'row'), may hold values from -6 to 6
- panels: float32 [2, 12288, 512], P(None, ('row', 'col')), may hold values from -0.06 to 0.06
- link_panels: float32 [1, 512, 512], P(None, 'row'), may hold values from -0.25 to 0.25
- diag_inverse: float32 [2, 512, 512], P(None, 'row'), may hold values from -0.25 to 0.25
- blocks: int32 [2, 48], replicated, may hold values from 0 to 95, as said below
Outputs:
- columns: float32 [2, 12288, 512], P(None, ('row', 'col'))
- diagonal: float32 [2, 512, 512], P(None, 'row', 'col')
Inputs may be any that keep to these rules, and one draw needn't show every extreme that they name: Each of the 2 rows names 48 different row blocks.
All inputs are finite; a program needn't handle non-finite values.
Results may differ from a plain program's by a relative error of at most 0.0001.
Values sent between devices are 32-bit elements; how exact they have to be, the bound alone decides.
No kernel may reach another device: no remote copies, remote signals or barrier semaphores. Data moves between devices by JAX's collectives and lax.ppermute only.
A program may use at most 128 MiB of HBM per device.

v0:
```python
import jax
import jax.numpy as jnp
from jax import lax
from jax.sharding import PartitionSpec as P

BLOCK = 128


def matmul(left, right):
    return jnp.dot(left, right, precision=lax.Precision.HIGHEST, preferred_element_type=jnp.float32)


def matmul_left_t(left, right):
    return lax.dot_general(
        left,
        right,
        (((0,), (0,)), ((), ())),
        precision=lax.Precision.HIGHEST,
        preferred_element_type=jnp.float32,
    )


def select_rows(values, row_block, chosen):
    hit = jnp.any(row_block[:, None] == chosen[None, :], axis=1)
    return jnp.where(hit[:, None], values, jnp.float32(0.0))


def body(ancestor, panels, link_panels, diag_inverse, blocks):
    row_count = lax.axis_size("row")
    col_count = lax.axis_size("col")
    row_index = lax.axis_index("row")
    col_index = lax.axis_index("col")
    resident_t = ancestor.reshape(ancestor.shape[0] * ancestor.shape[1], ancestor.shape[2])
    supernodes = panels.shape[0]
    rows_here = panels.shape[1]
    panel_width = panels.shape[2]
    rows_part = panel_width // row_count
    cols_part = panel_width // col_count
    first_row = (row_index * col_count + col_index) * rows_here
    row_block = (first_row + jnp.arange(rows_here, dtype=jnp.int32)) // BLOCK
    masked = jnp.stack(
        [select_rows(panels[number], row_block, blocks[number]) for number in range(supernodes)]
    )
    global_rows = row_index * rows_part + jnp.arange(rows_part, dtype=jnp.int32)
    lower_keep = jnp.arange(panel_width, dtype=jnp.int32)[None, :] <= global_rows[:, None]
    col_list = []
    diag_list = []
    prev_cols = None
    prev_full = None
    for supernode in range(supernodes):
        local_panel = masked[supernode]
        folded_one = matmul_left_t(
            resident_t, lax.all_gather(local_panel, "row", axis=0, tiled=True)
        )
        product = lax.psum_scatter(folded_one, "col", scatter_dimension=0, tiled=True)
        if supernode > 0:
            link = lax.all_gather(link_panels[supernode - 1], "row", axis=0, tiled=True)
        lowered = jnp.where(lower_keep, diag_inverse[supernode], jnp.float32(0.0))
        right_part = lax.dynamic_slice_in_dim(lowered, col_index * cols_part, cols_part, 1)
        share = matmul(lowered.T, right_part)
        if supernode == 0:
            cols_now = -product
            partial_value = -matmul(local_panel.T, cols_now)
        else:
            carried = matmul(prev_cols, link)
            cols_now = -(product + carried)
            partial_value = matmul(carried.T, local_panel) - matmul(local_panel.T, cols_now)
        current = lax.dynamic_slice_in_dim(partial_value, col_index * cols_part, cols_part, 1)
        partial_value = lax.dynamic_update_slice_in_dim(
            partial_value, current + share, col_index * cols_part, 1
        )
        diag_now = lax.psum(partial_value, ("row", "col"))
        if supernode > 0:
            diag_now = diag_now + matmul(link.T, matmul(prev_full, link))
        diag_block = lax.dynamic_slice(
            diag_now, (row_index * rows_part, col_index * cols_part), (rows_part, cols_part)
        )
        prev_full = diag_now
        col_list.append(cols_now)
        diag_list.append(diag_block)
        prev_cols = cols_now
    return (jnp.stack(col_list), jnp.stack(diag_list))


def solution(mesh):
    placed = (
        P(None, "col", "row"),
        P(None, ("row", "col"), None),
        P(None, "row", None),
        P(None, "row", None),
        P(),
    )
    return jax.shard_map(
        body,
        mesh=mesh,
        in_specs=placed,
        out_specs=(P(None, ("row", "col"), None), P(None, "row", "col")),
        check_vma=False,
    )
```

profile of v0, /device:TPU:0, one launch (start us, length us, event | category | flops | bytes accessed | tf_op | source)
XLA Modules:
  0.0 415.1 jit_solution(12558475619525118054)
XLA Ops:
  7.2 0.0 all-gather.5.cloned.1.call-start
  7.2 0.8 slice_bitcast_fusion
  8.0 0.1 compare_reduce_fusion.1
  8.1 2.7 bitcast_select_fusion.1
  10.8 0.0 all-gather.5.cloned.1.call-update
  10.8 0.0 all-gather.7.cloned.1.call-start
  10.9 0.7 all-gather.7.cloned.1.call-update
  11.6 0.0 all-gather.9.cloned.1.call-start
  11.6 0.7 all-gather.9.cloned.1.call-update
  12.3 0.0 reduce-scatter.3.cloned.1.call-start
  12.4 66.0 %all-gather.5.cloned.1.call-done = f32[3072,512]{1,0:T(8,128)} async-done(((f32[384,512]{1,0:T(8,128)}), f32[3072,512]{1,0:T(8,128)}) %all-gather.5.cloned.1.call-update) | async-done | bytes 6291472 | tf_op jit(solution)/shard_map/all_gather | solution.py:53
  78.4 35.4 %convolution_bitcast_fusion.1 = f32[1536,512]{0,1:T(8,128)} fusion(f32[3072,512]{1,0:T(8,128)} %all-gather.5.cloned.1.call-done, f32[3072,1536]{1,0:T(8,128)} %bitcast.46), kind=kOutput, calls=%fused_computation.1 | convolution fusion | flops 28991029248 | bytes 28311552 | tf_op jit(solution)/shard_map/dot_general | solution.py:14
  113.8 0.0 reduce-scatter.3.cloned.1.call-update
  113.8 0.0 copy-start.5
  113.8 0.2 reduce-scatter.5.cloned.1.call-start
  114.0 29.4 %all-gather.7.cloned.1.call-done = f32[3072,512]{1,0:T(8,128)} async-done(((f32[384,512]{1,0:T(8,128)}), f32[3072,512]{1,0:T(8,128)}) %all-gather.7.cloned.1.call-update) | async-done | bytes 6291472 | tf_op jit(solution)/shard_map/all_gather | solution.py:53
  143.4 35.5 %convolution_bitcast_fusion = f32[1536,512]{0,1:T(8,128)} fusion(f32[3072,512]{1,0:T(8,128)} %all-gather.7.cloned.1.call-done, f32[3072,1536]{1,0:T(8,128)} %bitcast.47), kind=kOutput, calls=%fused_computation | convolution fusion | flops 28991029248 | bytes 28311552 | tf_op jit(solution)/shard_map/dot_general | solution.py:14
  178.9 0.0 copy-start.2
  178.9 0.0 copy-start
  178.9 0.0 reduce-scatter.5.cloned.1.call-update
  178.9 0.3 all-reduce.3.cloned.1.call-start
  179.2 0.0 copy-done.5
  179.2 0.1 bitcast_select_fusion.2
  179.3 0.0 all-gather.9.cloned.1.call-done
  179.3 32.9 %reduce-scatter.3.cloned.1.call-done = f32[384,512]{0,1:T(8,128)} async-done(((f32[1536,512]{0,1:T(8,128)}), f32[384,512]{0,1:T(8,128)}) %reduce-scatter.3.cloned.1.call-update) | async-done | bytes 786448 | tf_op jit(solution)/shard_map/reduce_scatter | solution.py:55
  212.2 2.9 fusion.5
  215.2 1.2 copy.9
  216.4 0.0 copy-done.2
  216.4 0.0 copy-start.3
  216.4 4.9 %convolution_negate_fusion = f32[512,512]{1,0:T(8,128)} fusion(f32[384,512]{1,0:T(8,128)S(1)} %copy-done.2, f32[384,512]{0,1:T(8,128)} %reduce-scatter.3.cloned.1.call-done), kind=kOutput, calls=%fused_computation.5 | convolution fusion | flops 1208418304 | bytes 2621440 | tf_op jit(solution)/shard_map/dot_general | solution.py:10
  221.3 2.4 fusion.1
  223.6 0.0 copy-done
  223.6 2.8 fusion.18
  226.4 32.6 %reduce-scatter.5.cloned.1.call-done = f32[384,512]{0,1:T(8,128)} async-done(((f32[1536,512]{0,1:T(8,128)}), f32[384,512]{0,1:T(8,128)}) %reduce-scatter.5.cloned.1.call-update) | async-done | bytes 786448 | tf_op jit(solution)/shard_map/reduce_scatter | solution.py:55
  259.1 0.0 copy-start.4
  259.1 5.5 %convolution_subtract_fusion = f32[512,512]{1,0:T(8,128)} fusion(f32[512,512]{1,0:T(8,128)} %fusion.18, f32[384,512]{1,0:T(8,128)S(1)} %copy-done, f32[384,512]{0,1:T(8,128)} %reduce-scatter.5.cloned.1.call-done, f32[384,512]{0,1:T(8,128)} %copy.9), kind=kOutput, calls=%fused_computation.3 | convolution fusion | flops 1208614912 | bytes 4456448 | tf_op jit(solution)/shard_map/dot_general | solution.py:10
  264.5 2.3 fusion
  266.8 0.0 copy-start.1
  266.8 0.0 all-reduce.3.cloned.1.call-update
  266.8 0.0 copy-done.3
  266.8 0.1 negate_bitcast_fusion
  266.9 0.0 copy-done.4
  266.9 1.3 fusion.9
  268.2 0.1 pad_maximum_fusion
  268.3 1.6 copy.10
  269.9 131.7 %all-reduce.3.cloned.1.call-done = (f32[512,512]{1,0:T(8,128)}, f32[512,512]{1,0:T(8,128)}) async-done(((f32[512,512]{1,0:T(8,128)}, f32[512,512]{1,0:T(8,128)}), (f32[512,512]{1,0:T(8,128)}, f32[512,512]{1,0:T(8,128)})) %all-reduce.3.cloned.1.call-update) | async-done | bytes 2097168 | tf_op jit(solution)/shard_map/psum | solution.py:72
  401.6 0.0 copy-done.1
  401.6 3.3 fusion.3
  404.9 1.9 convolution_bitcast_fusion.2
  406.8 0.8 fusion.10
  407.6 0.6 pad_maximum_fusion.1
  (2 shorter events, 0.0 us)
Async XLA Ops:
  7.2 71.2 %all-gather.5.cloned.1.call-start = ((), (), s32[]{:S(2)}) async-start(), calls=%async_computation.2 | async-start | bytes 7077888 | tf_op jit(solution)/shard_map/all_gather | solution.py:53
  10.8 132.6 %all-gather.7.cloned.1.call-start = ((), (), s32[]{:S(2)}) async-start(), calls=%async_computation.4 | async-start | bytes 7077888 | tf_op jit(solution)/shard_map/all_gather | solution.py:53
  11.6 167.7 %all-gather.9.cloned.1.call-start = ((), (), s32[]{:S(2)}) async-start(), calls=%async_computation.6 | async-start | bytes 1179648 | tf_op jit(solution)/shard_map/all_gather | solution.py:57
  12.3 199.9 %reduce-scatter.3.cloned.1.call-start = ((), (), s32[]{:S(2)}) async-start(), calls=%async_computation.3 | async-start | bytes 3932160 | tf_op jit(solution)/shard_map/reduce_scatter | solution.py:55
  113.8 65.4 %copy-start.5 = (f32[2,64,512]{2,1,0:T(8,128)S(1)}, f32[2,64,512]{2,1,0:T(8,128)}, u32[]{:S(2)}) copy-start(f32[2,64,512]{2,1,0:T(8,128)} %param.8) | copy-start | bytes 786436
  113.8 145.2 %reduce-scatter.5.cloned.1.call-start = ((), (), s32[]{:S(2)}) async-start(), calls=%async_computation.5 | async-start | bytes 3932160 | tf_op jit(solution)/shard_map/reduce_scatter | solution.py:55
  178.9 37.5 %copy-start.2 = (f32[384,512]{1,0:T(8,128)S(1)}, f32[384,512]{1,0:T(8,128)}, u32[]{:S(2)}) copy-start(f32[384,512]{1,0:T(8,128)} %get-tuple-element.10) | copy-start | bytes 2359300
  178.9 44.8 %copy-start = (f32[384,512]{1,0:T(8,128)S(1)}, f32[384,512]{1,0:T(8,128)}, u32[]{:S(2)}) copy-start(f32[384,512]{1,0:T(8,128)} %get-tuple-element.11) | copy-start | bytes 2359300
  178.9 222.7 %all-reduce.3.cloned.1.call-start = ((), (), s32[]{:S(2)}) async-start(), calls=%async_computation.7 | async-start | bytes 4194304 | tf_op jit(solution)/shard_map/psum | solution.py:72
  216.4 50.5 %copy-start.3 = (f32[384,512]{0,1:T(8,128)S(1)}, f32[384,512]{0,1:T(8,128)}, u32[]{:S(2)}) copy-start(f32[384,512]{0,1:T(8,128)} %reduce-scatter.3.cloned.1.call-done) | copy-start | bytes 2359300
  259.1 7.9 %copy-start.4 = (f32[384,512]{0,1:T(8,128)S(1)}, f32[384,512]{0,1:T(8,128)}, u32[]{:S(2)}) copy-start(f32[384,512]{0,1:T(8,128)} %reduce-scatter.5.cloned.1.call-done) | copy-start | bytes 2359300
  266.8 134.8 %copy-start.1 = (f32[1,512,512]{2,1,0:T(8,128)S(1)}, f32[1,512,512]{2,1,0:T(8,128)}, u32[]{:S(2)}) copy-start(f32[1,512,512]{2,1,0:T(8,128)} %all-gather.9.cloned.1.call-done) | copy-start | bytes 3145732
Sparse Core Ops, SparseCore 0:
  10.9 67.4 all-gather.4
  80.0 63.3 all-gather.6
  145.0 20.8 all-gather.8
  168.8 43.4 reduce-scatter.2
  215.1 43.9 reduce-scatter.4
  267.0 134.5 all-reduce.2
where the time goes:
time: 416 us; the launch traced here: 415 us
  waiting for transfers between devices  294 us (71%)
  matrix products  96.8 us (23%)
  between operations  14.2 us (3%)
  other arithmetic  5.77 us (1%)
    psum x1, waiting for transfers between devices, body(): diag_now = lax.psum(partial_value, ('row', 'col'))  132 us
    all_gather x2, waiting for transfers between devices, body(): lax.all_gather(local_panel, 'row', axis=0, tiled=True)  95.4 us
    dot_general x2, matrix products, matmul_left_t(): lax.dot_general(left, right, (((0,), (0,)), ((), ())), precision=lax.Prec...  70.8 us
    reduce_scatter x2, waiting for transfers between devices, body(): lax.psum_scatter(folded_one, 'col', scatter_dimension=0, tiled=True)  65.6 us
    dot_general x8, matrix products, matmul(): jnp.dot(left, right, precision=lax.Precision.HIGHEST, preferred_element_t...  26 us
  transfers between devices with their start and end apart: 6, of which 5 were waited for; matrix products, arithmetic and copies ran while one was open for 21% of the time, Pallas kernels for 0%

commit v1 on v0

v1 whole, which is shorter than its diff:
```python
import jax
import jax.numpy as jnp
from jax import lax
from jax.experimental import pallas as pl
from jax.experimental.pallas import tpu as pltpu
from jax.sharding import PartitionSpec as P

BLOCK = 128
LANES = 128
HIGH = lax.Precision.HIGH
F32 = jnp.float32
BF16 = jnp.bfloat16


def matmul(left, right):
    return jnp.dot(left, right, precision=HIGH, preferred_element_type=F32)


def matmul_left_t(left, right):
    return lax.dot_general(
        left, right, (((0,), (0,)), ((), ())), precision=HIGH, preferred_element_type=F32
    )


def select_rows(values, row_block, chosen):
    hit = jnp.any(row_block[:, None] == chosen[None, :], axis=1)
    return jnp.where(hit[:, None], values, jnp.float32(0.0))


def take(values, index, axis):
    return lax.dynamic_index_in_dim(values, index, axis, keepdims=False)


def split_two(values):
    high = values.astype(BF16)
    low = (values - high.astype(F32)).astype(BF16)
    return high, low


def product_kernel(count, line, parts, rows, picks, per_group, *refs):
    chosen_ref, place_ref, resident_ref = refs[:3]
    pieces = refs[3 : 3 + 2 * line * parts]
    outs = refs[3 + 2 * line * parts : 3 + 2 * line * parts + count]
    panel_ref, resident_buf, ids_ref, panel_sem, resident_sem = refs[-5:]
    place, core, col = place_ref[0], place_ref[1], place_ref[2]
    width = panel_ref.shape[1]
    part = width // parts
    copies = []
    for hop in range(line):
        source = (place + line - hop) % line
        for other in range(2):
            group = source * 2 + (core if other == 0 else 1 - core)
            for p in range(parts):
                copies.append(
                    pltpu.make_async_copy(
                        pieces[(hop * 2 + other) * parts + p].at[pl.ds(0, rows), :],
                        panel_ref.at[pl.ds(group * rows, rows), pl.ds(p * part, part)],
                        panel_sem.at[len(copies)],
                    )
                )
    for copy in copies:
        copy.start()

    def note(i, found):
        block = chosen_ref[i]
        group = block // per_group
        inner = block % per_group
        mine = inner // (rows // BLOCK) == col

        @pl.when(mine)
        def _():
            ids_ref[found] = group * (rows // BLOCK) + inner % (rows // BLOCK)

        return found + mine.astype(jnp.int32)

    found = lax.fori_loop(0, picks, note, jnp.int32(0))
    ids_ref[found] = ids_ref[jnp.maximum(found - 1, 0)]
    pairs = (found + 1) // 2

    def fetch(pair, slot):
        return [
            pltpu.make_async_copy(
                resident_ref.at[pl.ds(ids_ref[2 * pair + k] * BLOCK, BLOCK), :],
                resident_buf.at[slot, pl.ds(k * BLOCK, BLOCK), :],
                resident_sem.at[slot, k],
            )
            for k in range(2)
        ]

    @pl.when(pairs > 0)
    def _():
        for copy in fetch(0, 0):
            copy.start()

    for out in outs:
        out[...] = jnp.zeros(out.shape, F32)
    for copy in copies:
        copy.wait()

    def step(pair, carry):
        slot = pair % 2

        @pl.when(pair + 1 < pairs)
        def _():
            for copy in fetch(pair + 1, 1 - slot):
                copy.start()

        first = panel_ref[pl.ds(pl.multiple_of(ids_ref[2 * pair] * BLOCK, BLOCK), BLOCK), :]
        second = panel_ref[pl.ds(pl.multiple_of(ids_ref[2 * pair + 1] * BLOCK, BLOCK), BLOCK), :]
        second = jnp.where(2 * pair + 1 < found, second, jnp.float32(0.0))
        high, low = split_two(jnp.concatenate([first, second], axis=0))
        right = jnp.concatenate([high, low, high], axis=0)
        for copy in fetch(pair, slot):
            copy.wait()
        for j in range(count):
            start = pl.multiple_of((col ^ j) * rows, LANES)
            high, low = split_two(resident_buf[slot, :, pl.ds(start, rows)])
            left = jnp.concatenate([high, high, low], axis=0)
            outs[j][...] += lax.dot_general(
                left, right, (((0,), (0,)), ((), ())), preferred_element_type=F32
            )
        return carry

    lax.fori_loop(0, pairs, step, 0)


def fold(resident_t, pieces, parts, chosen, position, line, col_count):
    place, core, col = position
    rows = resident_t.shape[1] // col_count
    width = sum(piece.shape[1] for piece in pieces[0][0])
    if rows % LANES or rows % BLOCK:
        whole = jnp.zeros((line, 2, rows, width), F32)
        for hop in range(line):
            source = (place - hop) % line
            for other in range(2):
                value = jnp.concatenate(pieces[hop][other], axis=1)[:rows]
                side = core if other == 0 else 1 - core
                whole = lax.dynamic_update_slice(whole, value[None, None], (source, side, 0, 0))
        folded = matmul_left_t(resident_t, whole.reshape(-1, width))
        folded = folded.reshape(col_count, rows, width)
        return [take(folded, col ^ j, 0) for j in range(col_count)]
    flat = [piece for hop in pieces for side in hop for piece in side]
    picks = chosen.shape[0]
    per_group = rows * col_count // BLOCK

    def kernel(*refs):
        product_kernel(col_count, line, parts, rows, picks, per_group, *refs)

    smem = pl.BlockSpec(memory_space=pltpu.SMEM)
    hbm = pl.BlockSpec(memory_space=pl.ANY)
    return pl.pallas_call(
        kernel,
        out_shape=[jax.ShapeDtypeStruct((rows, width), F32)] * col_count,
        in_specs=[smem, smem, hbm] + [hbm] * len(flat),
        out_specs=[pl.BlockSpec(memory_space=pltpu.VMEM)] * col_count,
        scratch_shapes=[
            pltpu.VMEM((2 * line * rows, width), F32),
            pltpu.VMEM((2, 2 * BLOCK, resident_t.shape[1]), F32),
            pltpu.SMEM((picks + 2,), jnp.int32),
            pltpu.SemaphoreType.DMA((len(flat),)),
            pltpu.SemaphoreType.DMA((2, 2)),
        ],
        name="fold",
    )(chosen, jnp.stack(position).astype(jnp.int32), resident_t, *flat)


def body(ancestor, panels, link_panels, diag_inverse, blocks):
    row_count = lax.axis_size("row")
    col_count = lax.axis_size("col")
    row_index = lax.axis_index("row")
    col_index = lax.axis_index("col")
    line = row_count // 2
    place = row_index // 2
    core = row_index % 2
    resident_t = ancestor.reshape(ancestor.shape[0] * ancestor.shape[1], ancestor.shape[2])
    supernodes, rows_here, width = panels.shape
    rows_part = width // row_count
    cols_part = width // col_count
    share_rows = rows_part // col_count
    first_row = (row_index * col_count + col_index) * rows_here
    row_block = (first_row + jnp.arange(rows_here, dtype=jnp.int32)) // BLOCK
    swap = [(i, i ^ 1) for i in range(row_count)]

    def ring(hop):
        return [(i, (i + 2 * hop) % row_count) for i in range(row_count)]

    def near(j):
        return [(i, i ^ j) for i in range(col_count)]

    masked = [select_rows(panels[s], row_block, blocks[s]) for s in range(supernodes)]
    link_own = [
        lax.dynamic_slice_in_dim(link_panels[s], col_index * share_rows, share_rows, 0)
        for s in range(supernodes - 1)
    ]

    parts = 2
    part = width // parts
    position = (place, core, col_index)
    tie = lax.optimization_barrier

    def streams(s):
        values = []
        for p in range(parts):
            rows = [masked[s][:, p * part : (p + 1) * part]]
            if s + 1 < supernodes:
                rows.append(link_own[s][:, p * part : (p + 1) * part])
            values.append(jnp.concatenate(rows, axis=0))
        return values

    def both(values):
        return values, [lax.ppermute(value, "row", swap) for value in values]

    def shift(values):
        return [lax.ppermute(value, "row", ring(1)) for value in values]

    near_rows = [
        [masked[s]] + [lax.ppermute(masked[s], "col", near(j)) for j in range(1, col_count)]
        if s > 0
        else None
        for s in range(supernodes)
    ]
    near_rows = tuple(near_rows)

    gathered, folds = [], []
    ahead = streams(0)
    for s in range(supernodes):
        now = ahead
        hops = [both(now)]
        for hop in range(1, line):
            now = shift(now)
            if hop == 1 and s > 0:
                now, folds[s - 1] = tie((now, folds[s - 1]))
            hops.append(both(now))
            if hop == line - 2 and s + 1 < supernodes:
                ahead, _ = tie((streams(s + 1), now))
        if s + 1 < supernodes:
            hops, near_rows = tie((hops, near_rows))
        gathered.append(hops)
        folds.append(fold(resident_t, hops, parts, blocks[s], position, line, col_count))

    def link_whole(s):
        mine = jnp.zeros((line, 2, share_rows, width), F32)
        for hop in range(line):
            source = (place - hop) % line
            for other in range(2):
                value = jnp.concatenate([v[rows_here:] for v in gathered[s][hop][other]], axis=1)
                side = core if other == 0 else 1 - core
                mine = lax.dynamic_update_slice(mine, value[None, None], (source, side, 0, 0))
        mine = mine.reshape(row_count, 1, share_rows, width)
        whole = jnp.zeros((row_count, col_count, share_rows, width), F32)
        for j in range(col_count):
            value = mine if j == 0 else lax.ppermute(mine, "col", near(j))
            whole = lax.dynamic_update_slice(whole, value, (0, col_index ^ j, 0, 0))
        return whole.reshape(width, width)

    links = [link_whole(s) for s in range(supernodes - 1)]

    global_rows = row_index * rows_part + col_index * share_rows + jnp.arange(share_rows, dtype=jnp.int32)
    keep = jnp.arange(width, dtype=jnp.int32)[None, :] <= global_rows[:, None]

    def reduce_diag(partial):
        count = partial.shape[0]
        view = partial.reshape(count, line, 2, rows_part, width)
        theirs = take(view, 1 - core, 2)
        view = take(view, core, 2) + lax.ppermute(theirs, "row", swap)
        total = take(view, place, 1)
        for hop in range(1, line):
            target = (place + hop) % line
            total = total + lax.ppermute(take(view, target, 1), "row", ring(hop))
        view = total.reshape(count, rows_part, col_count, cols_part)
        total = take(view, col_index, 2)
        for j in range(1, col_count):
            total = total + lax.ppermute(take(view, col_index ^ j, 2), "col", near(j))
        return total

    col_list, partials = [], []
    for s in range(supernodes):
        folded = folds[s]
        slab = lax.dynamic_slice_in_dim(diag_inverse[s], col_index * share_rows, share_rows, 0)
        slab = jnp.where(keep, slab, jnp.float32(0.0))
        partial = matmul_left_t(slab, slab)
        product = folded[0]
        for j in range(1, col_count):
            product = product + lax.ppermute(folded[j], "col", near(j))
        if s == 0:
            cols_now = -product
            partial = partial - matmul_left_t(masked[s], cols_now)
        else:
            link = links[s - 1]
            carried = matmul(col_list[-1], link)
            cols_now = -(product + carried)
            partial = partial + matmul_left_t(carried, masked[s])
            partial = partial + matmul_left_t(masked[s], carried)
            partial = partial + matmul_left_t(link, matmul(partials[-1], link))
            for j in range(col_count):
                partial = partial + matmul_left_t(near_rows[s][j], folded[j])
        col_list.append(cols_now)
        partials.append(partial)
    return (jnp.stack(col_list), reduce_diag(jnp.stack(partials)))


def solution(mesh):
    placed = (
        P(None, "col", "row"),
        P(None, ("row", "col"), None),
        P(None, "row", None),
        P(None, "row", None),
        P(),
    )
    return jax.shard_map(
        body,
        mesh=mesh,
        in_specs=placed,
        out_specs=(P(None, ("row", "col"), None), P(None, "row", "col")),
        check_vma=False,
    )
```

time: 416 us -> 238 us (0.57)
  waiting for transfers between devices: 294 us -> 115 us
  matrix products: 96.8 us -> 19.2 us
  starting transfers between devices: 0.64 us -> 42.3 us
  Pallas kernels: 0 us -> 29.6 us
  local copies, waits for them, and re-layouts: 3.58 us -> 18.1 us
  between operations: 14.2 us -> 1.4 us
  other arithmetic: 5.77 us -> 10.8 us
    psum x1 -> x0, waiting for transfers between devices: 132 us -> none  [body(): diag_now = lax.psum(partial_value, ('row', 'col'))]
    ppermute x0 -> x47, waiting for transfers between devices: none -> 115 us  [the longest x12 56.9 us: shift(): return [lax.ppermute(value, 'row', ring(1)) for value in values]]
    all_gather x3 -> x0, waiting for transfers between devices: 95.4 us -> none  [the longest x2 95.4 us: body(): lax.all_gather(local_panel, 'row', axis=0, tiled=True)]
    dot_general x10 -> x12, matrix products: 96.8 us -> 19.2 us  [the longest x10 17.3 us: matmul_left_t(): lax.dot_general(left, right, (((0,), (0,)), ((), ())), precision=HIGH, pr...]
    reduce_scatter x2 -> x0, waiting for transfers between devices: 65.6 us -> none  [body(): lax.psum_scatter(folded_one, 'col', scatter_dimension=0, tiled=True)]
    ppermute x0 -> x47, starting transfers between devices: none -> 42.3 us  [the longest x6 12.7 us: body(): product = product + lax.ppermute(folded[j], 'col', near(j))]
    pallas_call x0 -> x2, Pallas kernels: none -> 29.6 us  [fold(): pl.pallas_call(kernel, out_shape=[jax.ShapeDtypeStruct((rows, width), F32...]
    slice x0 -> x21, local copies, waits for them, and re-layouts: none -> 9.19 us  [the longest x17 6.49 us: link_whole(): v[rows_here:]]
  transfers between devices with their start and end apart: 6 -> 47, of which waited for: 5 -> 15; matrix products, arithmetic and copies ran while one was open for 21% -> 13% of each run, Pallas kernels for 0% -> 7%
where the time goes in v1:
time: 238 us; the launch traced here: 236 us
  waiting for transfers between devices  115 us (48%)
  starting transfers between devices  42.3 us (18%)
  Pallas kernels  29.6 us (12%)
  matrix products  19.2 us (8%)
  local copies, waits for them, and re-layouts  18.1 us (8%)
  other arithmetic  10.8 us (5%)
    ppermute x12, waiting for transfers between devices, shift(): return [lax.ppermute(value, 'row', ring(1)) for value in values]  56.9 us
    ppermute x6, waiting for transfers between devices, body(): product = product + lax.ppermute(folded[j], 'col', near(j))  39.4 us
    pallas_call x2, Pallas kernels, fold(): pl.pallas_call(kernel, out_shape=[jax.ShapeDtypeStruct((rows, width), F32...  29.6 us
    dot_general x10, matrix products, matmul_left_t(): lax.dot_general(left, right, (((0,), (0,)), ((), ())), precision=HIGH, pr...  17.3 us
    ppermute x3, waiting for transfers between devices, body(): lax.ppermute(masked[s], 'col', near(j))  17.1 us
    ppermute x6, starting transfers between devices, body(): product = product + lax.ppermute(folded[j], 'col', near(j))  12.7 us
    ppermute x12, starting transfers between devices, shift(): return [lax.ppermute(value, 'row', ring(1)) for value in values]  12 us
    slice x17, local copies, waits for them, and re-layouts, link_whole(): v[rows_here:]  6.49 us
  transfers between devices with their start and end apart: 47, of which 15 were waited for; matrix products, arithmetic and copies ran while one was open for 13% of the time, Pallas kernels for 7%

profile of v1, /device:TPU:0, one launch (start us, length us, event | category | flops | bytes accessed | tf_op | source)
XLA Modules:
  0.0 236.1 jit_solution(9834588536127283832)
XLA Ops:
  0.7 0.8 slice_bitcast_fusion.1
  1.7 1.6 bitcast_select_fusion
  3.4 3.1 %collective-permute-start = (f32[400,256]{1,0:T(8,128)S(1)}, f32[400,256]{1,0:T(8,128)S(1)}, u32[]{:S(2)}, u32[]{:S(2)}) collective-permute-start(f32[400,256]{1,0:T(8,128)S(1)} %pad_maximum_fusion.1.refs_3_), channel_id=1, source_target_pairs={{0,8},{4,12},{8,16},{12,20},{16,24},{20,28},{24,0},{28,4},{1,9},{5... | collective-permute-start | bytes 1228808 | tf_op jit(solution)/shard_map/ppermute | solution.py:214
  6.5 1.6 collective-permute-start.2
  8.7 1.5 collective-permute-start.16
  10.1 8.7 %collective-permute-done.refs_7_ = f32[400,256]{1,0:T(8,128)S(1)} collective-permute-done((f32[400,256]{1,0:T(8,128)S(1)}, f32[400,256]{1,0:T(8,128)S(1)}, u32[]{:S(2)}, u32[]{:S(2)}) %collective-permute-start) | collective-permute-done | bytes 409632 | tf_op jit(solution)/shard_map/ppermute | solution.py:214
  18.8 8.8 %collective-permute-done.2.refs_8_ = f32[400,256]{1,0:T(8,128)S(1)} collective-permute-done((f32[400,256]{1,0:T(8,128)S(1)}, f32[400,256]{1,0:T(8,128)S(1)}, u32[]{:S(2)}, u32[]{:S(2)}) %collective-permute-start.2) | collective-permute-done | bytes 409632 | tf_op jit(solution)/shard_map/ppermute | solution.py:214
  27.6 1.8 collective-permute-start.17
  29.4 1.4 collective-permute-start.18
  30.9 5.6 %collective-permute-done.1.refs_11_ = f32[400,256]{1,0:T(8,128)} collective-permute-done((f32[400,256]{1,0:T(8,128)S(1)}, f32[400,256]{1,0:T(8,128)}, u32[]{:S(2)}, u32[]{:S(2)}) %collective-permute-start.1) | collective-permute-done | bytes 409632 | tf_op jit(solution)/shard_map/ppermute | solution.py:214
  36.5 8.8 %collective-permute-done.3.refs_12_ = f32[400,256]{1,0:T(8,128)} collective-permute-done((f32[400,256]{1,0:T(8,128)S(1)}, f32[400,256]{1,0:T(8,128)}, u32[]{:S(2)}, u32[]{:S(2)}) %collective-permute-start.3) | collective-permute-done | bytes 409632 | tf_op jit(solution)/shard_map/ppermute | solution.py:214
  45.2 17.1 %collective-permute-done.17 = f32[384,512]{1,0:T(8,128)S(1)} collective-permute-done((f32[384,512]{1,0:T(8,128)S(1)}, f32[384,512]{1,0:T(8,128)S(1)}, u32[]{:S(2)}, u32[]{:S(2)}) %collective-permute-start.17) | collective-permute-done | bytes 786464 | tf_op jit(solution)/shard_map/ppermute | solution.py:217
  64.8 0.9 fusion.38
  66.5 1.6 collective-permute-start.5
  68.1 0.7 slice.103
  68.8 0.7 slice.105
  69.5 0.7 slice.104
  70.3 0.7 slice.107
  74.8 1.6 collective-permute-start.37
  77.0 1.7 fusion.39
  78.7 1.5 collective-permute-start.38
  80.7 15.5 %fold.2 = (f32[384,512]{1,0:T(8,128)}, f32[384,512]{1,0:T(8,128)}, f32[384,512]{1,0:T(8,128)}, f32[384,512]{1,0:T(8,128)}) custom-call(s32[48]{0:T(128)} %copy-done.35, s32[3]{0:T(128)} %pad_add_fusion.refs_1_, f32[3072,1536]{1,0:T(8,128)} %bitcast.105, f32[400,256]{1,0:T(8,128)} %copy-done.9, f32[400,256]{1,0:T(8,128)} %copy-done.10, ...), custom_call_target="tpu_custom_call" | custom-call | tf_op jit(solution)/shard_map/fold/pallas_call | solution.py:151
  96.2 4.1 %collective-permute-start.21 = (f32[384,512]{1,0:T(8,128)}, f32[384,512]{1,0:T(8,128)S(1)}, u32[]{:S(2)}, u32[]{:S(2)}) collective-permute-start(f32[384,512]{1,0:T(8,128)} %get-tuple-element.63), channel_id=1, source_target_pairs={{0,3},{1,2},{2,1},{3,0},{4,7},{5,6},{6,5},{7,4},{8,11},{9,10},{10,... | collective-permute-start | bytes 2359304 | tf_op jit(solution)/shard_map/ppermute | solution.py:284
  100.9 2.5 %fusion.20 = f32[512,512]{1,0:T(8,128)} fusion(f32[1,64,512]{2,1,0:T(8,128)} %get-tuple-element.90, s32[]{:T(128)S(6)} %select_n.139, s32[16]{0:T(128)S(1)} %iota_add_fusion.1), kind=kOutput, calls=%fused_computation.51 | convolution fusion | flops 25182208 | bytes 1081412 | tf_op jit(solution)/shard_map/dot_general | solution.py:20
  103.4 1.5 fusion.18
  105.0 2.2 collective-permute-start.26
  107.7 1.0 constant_dynamic-update-slice_fusion.2
  108.6 1.0 constant_dynamic-update-slice_fusion.1
  109.6 1.0 constant_dynamic-update-slice_fusion
  110.6 8.4 %collective-permute-done.26.refs_11_ = f32[384,256]{1,0:T(8,128)S(1)} collective-permute-done((f32[384,256]{1,0:T(8,128)}, f32[384,256]{1,0:T(8,128)S(1)}, u32[]{:S(2)}, u32[]{:S(2)}) %collective-permute-start.26) | collective-permute-done | bytes 393248 | tf_op jit(solution)/shard_map/ppermute | solution.py:214
  119.0 5.7 %collective-permute-done.27.refs_12_ = f32[384,256]{1,0:T(8,128)S(1)} collective-permute-done((f32[384,256]{1,0:T(8,128)}, f32[384,256]{1,0:T(8,128)S(1)}, u32[]{:S(2)}, u32[]{:S(2)}) %collective-permute-start.27) | collective-permute-done | bytes 393248 | tf_op jit(solution)/shard_map/ppermute | solution.py:214
  125.3 8.6 %collective-permute-done.20 = f32[384,512]{1,0:T(8,128)S(1)} collective-permute-done((f32[384,512]{1,0:T(8,128)}, f32[384,512]{1,0:T(8,128)S(1)}, u32[]{:S(2)}, u32[]{:S(2)}) %collective-permute-start.20) | collective-permute-done | bytes 786464 | tf_op jit(solution)/shard_map/ppermute | solution.py:284
  133.9 2.1 collective-permute-start.30
  136.0 0.9 copy-done.17
  137.3 1.5 add_negate_fusion
  138.8 0.9 fusion.41
  140.3 1.1 convolution_subtract_fusion
  141.3 1.0 convolution_add_fusion.2
  142.4 1.1 convolution_add_fusion.1
  144.2 3.5 %collective-permute-done.30.refs_15_ = f32[384,256]{1,0:T(8,128)S(1)} collective-permute-done((f32[384,256]{1,0:T(8,128)S(1)}, f32[384,256]{1,0:T(8,128)S(1)}, u32[]{:S(2)}, u32[]{:S(2)}) %collective-permute-start.30) | collective-permute-done | bytes 393248 | tf_op jit(solution)/shard_map/ppermute | solution.py:214
  147.7 7.5 %collective-permute-done.31.refs_16_ = f32[384,256]{1,0:T(8,128)S(1)} collective-permute-done((f32[384,256]{1,0:T(8,128)S(1)}, f32[384,256]{1,0:T(8,128)S(1)}, u32[]{:S(2)}, u32[]{:S(2)}) %collective-permute-start.31) | collective-permute-done | bytes 393248 | tf_op jit(solution)/shard_map/ppermute | solution.py:214
  155.1 1.0 fusion.42
  156.2 2.0 convolution_add_fusion.3
  158.3 0.7 copy-done.30
  159.3 0.8 copy-done.33
  160.1 14.1 %fold.3 = (f32[384,512]{1,0:T(8,128)}, f32[384,512]{1,0:T(8,128)}, f32[384,512]{1,0:T(8,128)}, f32[384,512]{1,0:T(8,128)}) custom-call(s32[48]{0:T(128)} %copy-done.34, s32[3]{0:T(128)} %pad_add_fusion.refs_1_, f32[3072,1536]{1,0:T(8,128)} %bitcast.106, f32[384,256]{1,0:T(8,128)} %get-tuple-element.38.refs_3_, f32[384,256]{1,0:T(8,128)} %get-tuple-element.39.refs_4_, ...), custom_call_target="tpu_custom_call" | custom-call | tf_op jit(solution)/shard_map/fold/pallas_call | solution.py:151
  174.2 2.5 %fusion.45 = f32[512,512]{1,0:T(8,128)S(1)} fusion(f32[384,512]{1,0:T(8,128)} %copy-done.15, f32[384,512]{1,0:T(8,128)} %get-tuple-element.69), kind=kOutput, calls=%fused_computation.96 | convolution fusion | flops 603979776 | bytes 2621440 | tf_op jit(solution)/shard_map/dot_general | solution.py:20
  176.7 2.2 fusion.44
  179.0 2.3 fusion.43
  181.3 1.1 fusion.2
  182.5 1.2 fusion.4
  184.3 4.2 %collective-permute-start.36 = (f32[384,512]{1,0:T(8,128)}, f32[384,512]{1,0:T(8,128)}, u32[]{:S(2)}, u32[]{:S(2)}) collective-permute-start(f32[384,512]{1,0:T(8,128)} %get-tuple-element.69), channel_id=1, source_target_pairs={{0,3},{1,2},{2,1},{3,0},{4,7},{5,6},{6,5},{7,4},{8,11},{9,10},{10,... | collective-permute-start | bytes 2359304 | tf_op jit(solution)/shard_map/ppermute | solution.py:284
  188.4 2.3 collective-permute-start.35
  190.8 1.5 collective-permute-start.34
  192.2 1.6 fusion.7
  193.9 1.0 collective-permute-start.43
  194.9 0.9 collective-permute-start.42
  195.8 11.4 %collective-permute-done.36 = f32[384,512]{1,0:T(8,128)} collective-permute-done((f32[384,512]{1,0:T(8,128)}, f32[384,512]{1,0:T(8,128)}, u32[]{:S(2)}, u32[]{:S(2)}) %collective-permute-start.36) | collective-permute-done | bytes 786464 | tf_op jit(solution)/shard_map/ppermute | solution.py:284
  207.5 17.4 %collective-permute-done.35 = f32[384,512]{1,0:T(8,128)} collective-permute-done((f32[384,512]{1,0:T(8,128)}, f32[384,512]{1,0:T(8,128)}, u32[]{:S(2)}, u32[]{:S(2)}) %collective-permute-start.35) | collective-permute-done | bytes 786464 | tf_op jit(solution)/shard_map/ppermute | solution.py:284
  224.9 2.0 collective-permute-done.34
  226.9 2.1 negate_bitcast_fusion
  229.7 1.4 collective-permute-start.45
  231.2 1.8 collective-permute-start.44
  232.9 1.3 pad_maximum_fusion
  (170 shorter events, 16.2 us)
Async XLA Ops:
  3.2 3.3 %copy-start.3 = (f32[384,512]{1,0:T(8,128)}, f32[384,512]{1,0:T(8,128)S(1)}, u32[]{:S(2)}) copy-start(f32[384,512]{1,0:T(8,128)S(1)} %get-tuple-element.76) | copy-start | bytes 2359300
  3.3 71.3 %copy-start.9 = (f32[400,256]{1,0:T(8,128)}, f32[400,256]{1,0:T(8,128)S(1)}, u32[]{:S(2)}) copy-start(f32[400,256]{1,0:T(8,128)S(1)} %pad_maximum_fusion.1.refs_3_) | copy-start | bytes 1228804
  3.4 15.4 %collective-permute-start = (f32[400,256]{1,0:T(8,128)S(1)}, f32[400,256]{1,0:T(8,128)S(1)}, u32[]{:S(2)}, u32[]{:S(2)}) collective-permute-start(f32[400,256]{1,0:T(8,128)S(1)} %pad_maximum_fusion.1.refs_3_), channel_id=1, source_target_pairs={{0,8},{4,12},{8,16},{12,20},{16,24},{20,28},{24,0},{28,4},{1,9},{5... | collective-permute-start | bytes 1228808 | tf_op jit(solution)/shard_map/ppermute | solution.py:214
  6.5 72.2 %copy-start.10 = (f32[400,256]{1,0:T(8,128)}, f32[400,256]{1,0:T(8,128)S(1)}, u32[]{:S(2)}) copy-start(f32[400,256]{1,0:T(8,128)S(1)} %pad_maximum_fusion.2.refs_4_) | copy-start | bytes 1228804
  6.5 21.1 %collective-permute-start.2 = (f32[400,256]{1,0:T(8,128)S(1)}, f32[400,256]{1,0:T(8,128)S(1)}, u32[]{:S(2)}, u32[]{:S(2)}) collective-permute-start(f32[400,256]{1,0:T(8,128)S(1)} %pad_maximum_fusion.2.refs_4_), channel_id=1, source_target_pairs={{0,8},{4,12},{8,16},{12,20},{16,24},{20,28},{24,0},{28,4},{1,9},{5... | collective-permute-start | bytes 1228808 | tf_op jit(solution)/shard_map/ppermute | solution.py:214
  8.1 19.4 %collective-permute-start.6 = (f32[400,256]{1,0:T(8,128)S(1)}, f32[400,256]{1,0:T(8,128)S(1)}, u32[]{:S(2)}, u32[]{:S(2)}) collective-permute-start(f32[400,256]{1,0:T(8,128)S(1)} %pad_maximum_fusion.1.refs_3_), channel_id=1, source_target_pairs={{0,4},{4,0},{8,12},{12,8},{16,20},{20,16},{24,28},{28,24},{1,5},{5... | collective-permute-start | bytes 1228808 | tf_op jit(solution)/shard_map/ppermute | solution.py:211
  8.1 21.3 %collective-permute-start.7 = (f32[400,256]{1,0:T(8,128)S(1)}, f32[400,256]{1,0:T(8,128)S(1)}, u32[]{:S(2)}, u32[]{:S(2)}) collective-permute-start(f32[400,256]{1,0:T(8,128)S(1)} %pad_maximum_fusion.2.refs_4_), channel_id=1, source_target_pairs={{0,4},{4,0},{8,12},{12,8},{16,20},{20,16},{24,28},{28,24},{1,5},{5... | collective-permute-start | bytes 1228808 | tf_op jit(solution)/shard_map/ppermute | solution.py:211
  8.7 22.2 %collective-permute-start.16 = (f32[384,512]{1,0:T(8,128)S(1)}, f32[384,512]{1,0:T(8,128)S(1)}, u32[]{:S(2)}, u32[]{:S(2)}) collective-permute-start(f32[384,512]{1,0:T(8,128)S(1)} %get-tuple-element.70), channel_id=1, source_target_pairs={{0,1},{1,0},{2,3},{3,2},{4,5},{5,4},{6,7},{7,6},{8,9},{9,8},{10,11... | collective-permute-start | bytes 2359304 | tf_op jit(solution)/shard_map/ppermute | solution.py:217
  18.8 61.9 %copy-start.18 = (f32[400,256]{1,0:T(8,128)}, f32[400,256]{1,0:T(8,128)S(1)}, u32[]{:S(2)}) copy-start(f32[400,256]{1,0:T(8,128)S(1)} %collective-permute-done.refs_7_) | copy-start | bytes 1228804
  18.8 17.7 %collective-permute-start.1 = (f32[400,256]{1,0:T(8,128)S(1)}, f32[400,256]{1,0:T(8,128)}, u32[]{:S(2)}, u32[]{:S(2)}) collective-permute-start(f32[400,256]{1,0:T(8,128)S(1)} %collective-permute-done.refs_7_), channel_id=1, source_target_pairs={{0,8},{4,12},{8,16},{12,20},{16,24},{20,28},{24,0},{28,4},{1,9},{5... | collective-permute-start | bytes 1228808 | tf_op jit(solution)/shard_map/ppermute | solution.py:214
  27.6 53.1 %copy-start.19 = (f32[400,256]{1,0:T(8,128)}, f32[400,256]{1,0:T(8,128)S(1)}, u32[]{:S(2)}) copy-start(f32[400,256]{1,0:T(8,128)S(1)} %collective-permute-done.2.refs_8_) | copy-start | bytes 1228804
  27.6 17.7 %collective-permute-start.3 = (f32[400,256]{1,0:T(8,128)S(1)}, f32[400,256]{1,0:T(8,128)}, u32[]{:S(2)}, u32[]{:S(2)}) collective-permute-start(f32[400,256]{1,0:T(8,128)S(1)} %collective-permute-done.2.refs_8_), channel_id=1, source_target_pairs={{0,8},{4,12},{8,16},{12,20},{16,24},{20,28},{24,0},{28,4},{1,9},{5... | collective-permute-start | bytes 1228808 | tf_op jit(solution)/shard_map/ppermute | solution.py:214
  27.6 53.1 %copy-start.20 = (f32[400,256]{1,0:T(8,128)}, f32[400,256]{1,0:T(8,128)S(1)}, u32[]{:S(2)}) copy-start(f32[400,256]{1,0:T(8,128)S(1)} %collective-permute-done.6.refs_5_) | copy-start | bytes 1228804
  27.6 34.8 %collective-permute-start.17 = (f32[384,512]{1,0:T(8,128)S(1)}, f32[384,512]{1,0:T(8,128)S(1)}, u32[]{:S(2)}, u32[]{:S(2)}) collective-permute-start(f32[384,512]{1,0:T(8,128)S(1)} %get-tuple-element.70), channel_id=1, source_target_pairs={{0,2},{1,3},{2,0},{3,1},{4,6},{5,7},{6,4},{7,5},{8,10},{9,11},{10,... | collective-permute-start | bytes 2359304 | tf_op jit(solution)/shard_map/ppermute | solution.py:217
  29.4 51.3 %copy-start.21 = (f32[400,256]{1,0:T(8,128)}, f32[400,256]{1,0:T(8,128)S(1)}, u32[]{:S(2)}) copy-start(f32[400,256]{1,0:T(8,128)S(1)} %collective-permute-done.7.refs_6_) | copy-start | bytes 1228804
  29.4 33.0 %collective-permute-start.18 = (f32[384,512]{1,0:T(8,128)S(1)}, f32[384,512]{1,0:T(8,128)S(1)}, u32[]{:S(2)}, u32[]{:S(2)}) collective-permute-start(f32[384,512]{1,0:T(8,128)S(1)} %get-tuple-element.70), channel_id=1, source_target_pairs={{0,3},{1,2},{2,1},{3,0},{4,7},{5,6},{6,5},{7,4},{8,11},{9,10},{10,... | collective-permute-start | bytes 2359304 | tf_op jit(solution)/shard_map/ppermute | solution.py:217
  30.8 31.5 %copy-start.11 = (f32[384,512]{1,0:T(8,128)}, f32[384,512]{1,0:T(8,128)S(1)}, u32[]{:S(2)}) copy-start(f32[384,512]{1,0:T(8,128)S(1)} %collective-permute-done.16) | copy-start | bytes 2359300
  30.8 32.4 %collective-permute-start.8 = (f32[400,256]{1,0:T(8,128)S(1)}, f32[400,256]{1,0:T(8,128)S(1)}, u32[]{:S(2)}, u32[]{:S(2)}) collective-permute-start(f32[400,256]{1,0:T(8,128)S(1)} %collective-permute-done.refs_7_), channel_id=1, source_target_pairs={{0,4},{4,0},{8,12},{12,8},{16,20},{20,16},{24,28},{28,24},{1,5},{5... | collective-permute-start | bytes 1228808 | tf_op jit(solution)/shard_map/ppermute | solution.py:211
  36.5 27.9 %collective-permute-start.12 = (f32[400,256]{1,0:T(8,128)}, f32[400,256]{1,0:T(8,128)}, u32[]{:S(2)}, u32[]{:S(2)}) collective-permute-start(f32[400,256]{1,0:T(8,128)} %collective-permute-done.1.refs_11_), channel_id=1, source_target_pairs={{0,8},{4,12},{8,16},{12,20},{16,24},{20,28},{24,0},{28,4},{1,9},{5... | collective-permute-start | bytes 1228808 | tf_op jit(solution)/shard_map/ppermute | solution.py:214
  45.2 19.3 %collective-permute-start.13 = (f32[400,256]{1,0:T(8,128)}, f32[400,256]{1,0:T(8,128)}, u32[]{:S(2)}, u32[]{:S(2)}) collective-permute-start(f32[400,256]{1,0:T(8,128)} %collective-permute-done.3.refs_12_), channel_id=1, source_target_pairs={{0,8},{4,12},{8,16},{12,20},{16,24},{20,28},{24,0},{28,4},{1,9},{5... | collective-permute-start | bytes 1228808 | tf_op jit(solution)/shard_map/ppermute | solution.py:214
  62.4 3.4 %collective-permute-start.9 = (f32[400,256]{1,0:T(8,128)S(1)}, f32[400,256]{1,0:T(8,128)}, u32[]{:S(2)}, u32[]{:S(2)}) collective-permute-start(f32[400,256]{1,0:T(8,128)S(1)} %collective-permute-done.2.refs_8_), channel_id=1, source_target_pairs={{0,4},{4,0},{8,12},{12,8},{16,20},{20,16},{24,28},{28,24},{1,5},{5... | collective-permute-start | bytes 1228808 | tf_op jit(solution)/shard_map/ppermute | solution.py:211
  62.4 4.0 %collective-permute-start.10 = (f32[400,256]{1,0:T(8,128)}, f32[400,256]{1,0:T(8,128)}, u32[]{:S(2)}, u32[]{:S(2)}) collective-permute-start(f32[400,256]{1,0:T(8,128)} %collective-permute-done.1.refs_11_), channel_id=1, source_target_pairs={{0,4},{4,0},{8,12},{12,8},{16,20},{20,16},{24,28},{28,24},{1,5},{5... | collective-permute-start | bytes 1228808 | tf_op jit(solution)/shard_map/ppermute | solution.py:211
  63.5 4.5 %collective-permute-start.11 = (f32[400,256]{1,0:T(8,128)}, f32[400,256]{1,0:T(8,128)}, u32[]{:S(2)}, u32[]{:S(2)}) collective-permute-start(f32[400,256]{1,0:T(8,128)} %collective-permute-done.3.refs_12_), channel_id=1, source_target_pairs={{0,4},{4,0},{8,12},{12,8},{16,20},{20,16},{24,28},{28,24},{1,5},{5... | collective-permute-start | bytes 1228808 | tf_op jit(solution)/shard_map/ppermute | solution.py:211
  64.3 10.4 %slice-start = ((f32[400,256]{1,0:T(8,128)}), f32[16,256]{1,0:T(8,128)S(1)}, s32[]{:S(2)}) async-start(f32[400,256]{1,0:T(8,128)} %copy-done.22), calls=%async_computation | async-start | bytes 32768 | tf_op jit(solution)/shard_map/slice | solution.py:246
  64.3 3.7 %collective-permute-start.14 = (f32[400,256]{1,0:T(8,128)}, f32[400,256]{1,0:T(8,128)}, u32[]{:S(2)}, u32[]{:S(2)}) collective-permute-start(f32[400,256]{1,0:T(8,128)} %collective-permute-done.12.refs_15_), channel_id=1, source_target_pairs={{0,4},{4,0},{8,12},{12,8},{16,20},{20,16},{24,28},{28,24},{1,5},{5... | collective-permute-start | bytes 1228808 | tf_op jit(solution)/shard_map/ppermute | solution.py:211
  64.6 3.5 %collective-permute-start.15 = (f32[400,256]{1,0:T(8,128)}, f32[400,256]{1,0:T(8,128)}, u32[]{:S(2)}, u32[]{:S(2)}) collective-permute-start(f32[400,256]{1,0:T(8,128)} %collective-permute-done.13.refs_16_), channel_id=1, source_target_pairs={{0,4},{4,0},{8,12},{12,8},{16,20},{20,16},{24,28},{28,24},{1,5},{5... | collective-permute-start | bytes 1228808 | tf_op jit(solution)/shard_map/ppermute | solution.py:211
  65.8 30.4 %collective-permute-start.4 = (f32[384,256]{1,0:T(8,128)}, f32[384,256]{1,0:T(8,128)}, u32[]{:S(2)}, u32[]{:S(2)}) collective-permute-start(f32[384,256]{1,0:T(8,128)} %get-tuple-element.38.refs_3_), channel_id=1, source_target_pairs={{0,8},{4,12},{8,16},{12,20},{16,24},{20,28},{24,0},{28,4},{1,9},{5... | collective-permute-start | bytes 1179656 | tf_op jit(solution)/shard_map/ppermute | solution.py:214
  66.5 29.7 %collective-permute-start.5 = (f32[384,256]{1,0:T(8,128)}, f32[384,256]{1,0:T(8,128)}, u32[]{:S(2)}, u32[]{:S(2)}) collective-permute-start(f32[384,256]{1,0:T(8,128)} %get-tuple-element.39.refs_4_), channel_id=1, source_target_pairs={{0,8},{4,12},{8,16},{12,20},{16,24},{20,28},{24,0},{28,4},{1,9},{5... | collective-permute-start | bytes 1179656 | tf_op jit(solution)/shard_map/ppermute | solution.py:214
  74.8 25.5 %collective-permute-start.37 = (f32[8,1,16,512]{3,2,1,0:T(8,128)S(1)}, f32[8,1,16,512]{3,2,1,0:T(8,128)}, u32[]{:S(2)}, u32[]{:S(2)}) collective-permute-start(f32[8,1,16,512]{3,2,1,0:T(8,128)S(1)} %bitcast.115), channel_id=1, source_target_pairs={{0,1},{1,0},{2,3},{3,2},{4,5},{5,4},{6,7},{7,6},{8,9},{9,8},{10,11... | collective-permute-start | bytes 786440 | tf_op jit(solution)/shard_map/ppermute | solution.py:252
  78.7 26.3 %collective-permute-start.38 = (f32[8,1,16,512]{3,2,1,0:T(8,128)S(1)}, f32[8,1,16,512]{3,2,1,0:T(8,128)}, u32[]{:S(2)}, u32[]{:S(2)}) collective-permute-start(f32[8,1,16,512]{3,2,1,0:T(8,128)S(1)} %bitcast.116), channel_id=1, source_target_pairs={{0,2},{1,3},{2,0},{3,1},{4,6},{5,7},{6,4},{7,5},{8,10},{9,11},{10,... | collective-permute-start | bytes 786440 | tf_op jit(solution)/shard_map/ppermute | solution.py:252
  80.2 27.0 %collective-permute-start.39 = (f32[8,1,16,512]{3,2,1,0:T(8,128)S(1)}, f32[8,1,16,512]{3,2,1,0:T(8,128)}, u32[]{:S(2)}, u32[]{:S(2)}) collective-permute-start(f32[8,1,16,512]{3,2,1,0:T(8,128)S(1)} %bitcast.117), channel_id=1, source_target_pairs={{0,3},{1,2},{2,1},{3,0},{4,7},{5,6},{6,5},{7,4},{8,11},{9,10},{10,... | collective-permute-start | bytes 786440 | tf_op jit(solution)/shard_map/ppermute | solution.py:252
  96.2 28.6 %collective-permute-start.21 = (f32[384,512]{1,0:T(8,128)}, f32[384,512]{1,0:T(8,128)S(1)}, u32[]{:S(2)}, u32[]{:S(2)}) collective-permute-start(f32[384,512]{1,0:T(8,128)} %get-tuple-element.63), channel_id=1, source_target_pairs={{0,3},{1,2},{2,1},{3,0},{4,7},{5,6},{6,5},{7,4},{8,11},{9,10},{10,... | collective-permute-start | bytes 2359304 | tf_op jit(solution)/shard_map/ppermute | solution.py:284
  100.3 33.6 %collective-permute-start.20 = (f32[384,512]{1,0:T(8,128)}, f32[384,512]{1,0:T(8,128)S(1)}, u32[]{:S(2)}, u32[]{:S(2)}) collective-permute-start(f32[384,512]{1,0:T(8,128)} %get-tuple-element.62), channel_id=1, source_target_pairs={{0,2},{1,3},{2,0},{3,1},{4,6},{5,7},{6,4},{7,5},{8,10},{9,11},{10,... | collective-permute-start | bytes 2359304 | tf_op jit(solution)/shard_map/ppermute | solution.py:284
  100.3 35.7 %collective-permute-start.19 = (f32[384,512]{1,0:T(8,128)}, f32[384,512]{1,0:T(8,128)S(1)}, u32[]{:S(2)}, u32[]{:S(2)}) collective-permute-start(f32[384,512]{1,0:T(8,128)} %get-tuple-element.61), channel_id=1, source_target_pairs={{0,1},{1,0},{2,3},{3,2},{4,5},{5,4},{6,7},{7,6},{8,9},{9,8},{10,11... | collective-permute-start | bytes 2359304 | tf_op jit(solution)/shard_map/ppermute | solution.py:284
  104.9 32.4 %copy-start.16 = (f32[384,512]{1,0:T(8,128)S(1)}, f32[384,512]{1,0:T(8,128)}, u32[]{:S(2)}) copy-start(f32[384,512]{1,0:T(8,128)} %get-tuple-element.60) | copy-start | bytes 2359300
  105.0 14.0 %collective-permute-start.26 = (f32[384,256]{1,0:T(8,128)}, f32[384,256]{1,0:T(8,128)S(1)}, u32[]{:S(2)}, u32[]{:S(2)}) collective-permute-start(f32[384,256]{1,0:T(8,128)} %collective-permute-done.4.refs_7_), channel_id=1, source_target_pairs={{0,8},{4,12},{8,16},{12,20},{16,24},{20,28},{24,0},{28,4},{1,9},{5... | collective-permute-start | bytes 1179656 | tf_op jit(solution)/shard_map/ppermute | solution.py:214
  107.2 17.6 %collective-permute-start.27 = (f32[384,256]{1,0:T(8,128)}, f32[384,256]{1,0:T(8,128)S(1)}, u32[]{:S(2)}, u32[]{:S(2)}) collective-permute-start(f32[384,256]{1,0:T(8,128)} %collective-permute-done.5.refs_8_), channel_id=1, source_target_pairs={{0,8},{4,12},{8,16},{12,20},{16,24},{20,28},{24,0},{28,4},{1,9},{5... | collective-permute-start | bytes 1179656 | tf_op jit(solution)/shard_map/ppermute | solution.py:214
  119.0 24.5 %copy-start.23 = (f32[384,256]{1,0:T(8,128)}, f32[384,256]{1,0:T(8,128)S(1)}, u32[]{:S(2)}) copy-start(f32[384,256]{1,0:T(8,128)S(1)} %collective-permute-done.26.refs_11_) | copy-start | bytes 1179652
  119.0 24.4 %collective-permute-start.22 = (f32[384,256]{1,0:T(8,128)}, f32[384,256]{1,0:T(8,128)S(1)}, u32[]{:S(2)}, u32[]{:S(2)}) collective-permute-start(f32[384,256]{1,0:T(8,128)} %get-tuple-element.38.refs_3_), channel_id=1, source_target_pairs={{0,4},{4,0},{8,12},{12,8},{16,20},{20,16},{24,28},{28,24},{1,5},{5... | collective-permute-start | bytes 1179656 | tf_op jit(solution)/shard_map/ppermute | solution.py:211
  124.7 19.3 %copy-start.24 = (f32[384,256]{1,0:T(8,128)}, f32[384,256]{1,0:T(8,128)S(1)}, u32[]{:S(2)}) copy-start(f32[384,256]{1,0:T(8,128)S(1)} %collective-permute-done.27.refs_12_) | copy-start | bytes 1179652
  124.7 18.8 %collective-permute-start.23 = (f32[384,256]{1,0:T(8,128)}, f32[384,256]{1,0:T(8,128)S(1)}, u32[]{:S(2)}, u32[]{:S(2)}) collective-permute-start(f32[384,256]{1,0:T(8,128)} %get-tuple-element.39.refs_4_), channel_id=1, source_target_pairs={{0,4},{4,0},{8,12},{12,8},{16,20},{20,16},{24,28},{28,24},{1,5},{5... | collective-permute-start | bytes 1179656 | tf_op jit(solution)/shard_map/ppermute | solution.py:211
  124.8 19.3 %collective-permute-start.24 = (f32[384,256]{1,0:T(8,128)}, f32[384,256]{1,0:T(8,128)S(1)}, u32[]{:S(2)}, u32[]{:S(2)}) collective-permute-start(f32[384,256]{1,0:T(8,128)} %collective-permute-done.4.refs_7_), channel_id=1, source_target_pairs={{0,4},{4,0},{8,12},{12,8},{16,20},{20,16},{24,28},{28,24},{1,5},{5... | collective-permute-start | bytes 1179656 | tf_op jit(solution)/shard_map/ppermute | solution.py:211
  133.9 13.8 %collective-permute-start.30 = (f32[384,256]{1,0:T(8,128)S(1)}, f32[384,256]{1,0:T(8,128)S(1)}, u32[]{:S(2)}, u32[]{:S(2)}) collective-permute-start(f32[384,256]{1,0:T(8,128)S(1)} %collective-permute-done.26.refs_11_), channel_id=1, source_target_pairs={{0,8},{4,12},{8,16},{12,20},{16,24},{20,28},{24,0},{28,4},{1,9},{5... | collective-permute-start | bytes 1179656 | tf_op jit(solution)/shard_map/ppermute | solution.py:214
  136.9 18.2 %collective-permute-start.31 = (f32[384,256]{1,0:T(8,128)S(1)}, f32[384,256]{1,0:T(8,128)S(1)}, u32[]{:S(2)}, u32[]{:S(2)}) collective-permute-start(f32[384,256]{1,0:T(8,128)S(1)} %collective-permute-done.27.refs_12_), channel_id=1, source_target_pairs={{0,8},{4,12},{8,16},{12,20},{16,24},{20,28},{24,0},{28,4},{1,9},{5... | collective-permute-start | bytes 1179656 | tf_op jit(solution)/shard_map/ppermute | solution.py:214
  143.4 12.8 %copy-start.25 = (f32[384,256]{1,0:T(8,128)}, f32[384,256]{1,0:T(8,128)S(1)}, u32[]{:S(2)}) copy-start(f32[384,256]{1,0:T(8,128)S(1)} %collective-permute-done.22.refs_5_) | copy-start | bytes 1179652
  143.4 14.9 %collective-permute-start.25 = (f32[384,256]{1,0:T(8,128)}, f32[384,256]{1,0:T(8,128)S(1)}, u32[]{:S(2)}, u32[]{:S(2)}) collective-permute-start(f32[384,256]{1,0:T(8,128)} %collective-permute-done.5.refs_8_), channel_id=1, source_target_pairs={{0,4},{4,0},{8,12},{12,8},{16,20},{20,16},{24,28},{28,24},{1,5},{5... | collective-permute-start | bytes 1179656 | tf_op jit(solution)/shard_map/ppermute | solution.py:211
  143.5 12.7 %copy-start.26 = (f32[384,256]{1,0:T(8,128)}, f32[384,256]{1,0:T(8,128)S(1)}, u32[]{:S(2)}) copy-start(f32[384,256]{1,0:T(8,128)S(1)} %collective-permute-done.23.refs_6_) | copy-start | bytes 1179652
  143.5 14.7 %collective-permute-start.28 = (f32[384,256]{1,0:T(8,128)S(1)}, f32[384,256]{1,0:T(8,128)S(1)}, u32[]{:S(2)}, u32[]{:S(2)}) collective-permute-start(f32[384,256]{1,0:T(8,128)S(1)} %collective-permute-done.26.refs_11_), channel_id=1, source_target_pairs={{0,4},{4,0},{8,12},{12,8},{16,20},{20,16},{24,28},{28,24},{1,5},{5... | collective-permute-start | bytes 1179656 | tf_op jit(solution)/shard_map/ppermute | solution.py:211
  144.1 12.1 %copy-start.27 = (f32[384,256]{1,0:T(8,128)}, f32[384,256]{1,0:T(8,128)S(1)}, u32[]{:S(2)}) copy-start(f32[384,256]{1,0:T(8,128)S(1)} %collective-permute-done.24.refs_9_) | copy-start | bytes 1179652
  144.1 14.2 %collective-permute-start.29 = (f32[384,256]{1,0:T(8,128)S(1)}, f32[384,256]{1,0:T(8,128)S(1)}, u32[]{:S(2)}, u32[]{:S(2)}) collective-permute-start(f32[384,256]{1,0:T(8,128)S(1)} %collective-permute-done.27.refs_12_), channel_id=1, source_target_pairs={{0,4},{4,0},{8,12},{12,8},{16,20},{20,16},{24,28},{28,24},{1,5},{5... | collective-permute-start | bytes 1179656 | tf_op jit(solution)/shard_map/ppermute | solution.py:211
  147.7 8.6 %copy-start.28 = (f32[384,256]{1,0:T(8,128)}, f32[384,256]{1,0:T(8,128)S(1)}, u32[]{:S(2)}) copy-start(f32[384,256]{1,0:T(8,128)S(1)} %collective-permute-done.30.refs_15_) | copy-start | bytes 1179652
  147.7 10.7 %collective-permute-start.32 = (f32[384,256]{1,0:T(8,128)S(1)}, f32[384,256]{1,0:T(8,128)S(1)}, u32[]{:S(2)}, u32[]{:S(2)}) collective-permute-start(f32[384,256]{1,0:T(8,128)S(1)} %collective-permute-done.30.refs_15_), channel_id=1, source_target_pairs={{0,4},{4,0},{8,12},{12,8},{16,20},{20,16},{24,28},{28,24},{1,5},{5... | collective-permute-start | bytes 1179656 | tf_op jit(solution)/shard_map/ppermute | solution.py:211
  155.1 4.9 %collective-permute-start.33 = (f32[384,256]{1,0:T(8,128)S(1)}, f32[384,256]{1,0:T(8,128)}, u32[]{:S(2)}, u32[]{:S(2)}) collective-permute-start(f32[384,256]{1,0:T(8,128)S(1)} %collective-permute-done.31.refs_16_), channel_id=1, source_target_pairs={{0,4},{4,0},{8,12},{12,8},{16,20},{20,16},{24,28},{28,24},{1,5},{5... | collective-permute-start | bytes 1179656 | tf_op jit(solution)/shard_map/ppermute | solution.py:211
  183.8 8.5 %collective-permute-start.40 = (f32[2,4,64,512]{3,2,1,0:T(8,128)}, f32[2,4,64,512]{3,2,1,0:T(8,128)}, u32[]{:S(2)}, u32[]{:S(2)}) collective-permute-start(f32[2,4,64,512]{3,2,1,0:T(8,128)} %fusion.4), channel_id=1, source_target_pairs={{0,4},{4,0},{8,12},{12,8},{16,20},{20,16},{24,28},{28,24},{1,5},{5... | collective-permute-start | bytes 3145736 | tf_op jit(solution)/shard_map/ppermute | solution.py:265
  184.3 22.9 %collective-permute-start.36 = (f32[384,512]{1,0:T(8,128)}, f32[384,512]{1,0:T(8,128)}, u32[]{:S(2)}, u32[]{:S(2)}) collective-permute-start(f32[384,512]{1,0:T(8,128)} %get-tuple-element.69), channel_id=1, source_target_pairs={{0,3},{1,2},{2,1},{3,0},{4,7},{5,6},{6,5},{7,4},{8,11},{9,10},{10,... | collective-permute-start | bytes 2359304 | tf_op jit(solution)/shard_map/ppermute | solution.py:284
  188.4 36.5 %collective-permute-start.35 = (f32[384,512]{1,0:T(8,128)}, f32[384,512]{1,0:T(8,128)}, u32[]{:S(2)}, u32[]{:S(2)}) collective-permute-start(f32[384,512]{1,0:T(8,128)} %get-tuple-element.68), channel_id=1, source_target_pairs={{0,2},{1,3},{2,0},{3,1},{4,6},{5,7},{6,4},{7,5},{8,10},{9,11},{10,... | collective-permute-start | bytes 2359304 | tf_op jit(solution)/shard_map/ppermute | solution.py:284
  190.8 36.1 %collective-permute-start.34 = (f32[384,512]{1,0:T(8,128)}, f32[384,512]{1,0:T(8,128)}, u32[]{:S(2)}, u32[]{:S(2)}) collective-permute-start(f32[384,512]{1,0:T(8,128)} %get-tuple-element.67), channel_id=1, source_target_pairs={{0,1},{1,0},{2,3},{3,2},{4,5},{5,4},{6,7},{7,6},{8,9},{9,8},{10,11... | collective-permute-start | bytes 2359304 | tf_op jit(solution)/shard_map/ppermute | solution.py:284
  193.8 33.1 %copy-start.8 = (f32[384,512]{1,0:T(8,128)S(1)}, f32[384,512]{1,0:T(8,128)}, u32[]{:S(2)}) copy-start(f32[384,512]{1,0:T(8,128)} %get-tuple-element.66) | copy-start | bytes 2359300
  193.9 35.0 %collective-permute-start.43 = (f32[2,64,512]{2,1,0:T(8,128)S(1)}, f32[2,64,512]{2,1,0:T(8,128)S(1)}, u32[]{:S(2)}, u32[]{:S(2)}) collective-permute-start(f32[2,64,512]{2,1,0:T(8,128)S(1)} %get-tuple-element.79), channel_id=1, source_target_pairs={{0,24},{4,28},{8,0},{12,4},{16,8},{20,12},{24,16},{28,20},{1,25},{... | collective-permute-start | bytes 786440 | tf_op jit(solution)/shard_map/ppermute | solution.py:269
  194.9 34.0 %collective-permute-start.42 = (f32[2,64,512]{2,1,0:T(8,128)S(1)}, f32[2,64,512]{2,1,0:T(8,128)S(1)}, u32[]{:S(2)}, u32[]{:S(2)}) collective-permute-start(f32[2,64,512]{2,1,0:T(8,128)S(1)} %get-tuple-element.80), channel_id=1, source_target_pairs={{0,16},{4,20},{8,24},{12,28},{16,0},{20,4},{24,8},{28,12},{1,17},{... | collective-permute-start | bytes 786440 | tf_op jit(solution)/shard_map/ppermute | solution.py:269
  207.2 21.8 %collective-permute-start.41 = (f32[2,64,512]{2,1,0:T(8,128)S(1)}, f32[2,64,512]{2,1,0:T(8,128)S(1)}, u32[]{:S(2)}, u32[]{:S(2)}) collective-permute-start(f32[2,64,512]{2,1,0:T(8,128)S(1)} %get-tuple-element.78), channel_id=1, source_target_pairs={{0,8},{4,12},{8,16},{12,20},{16,24},{20,28},{24,0},{28,4},{1,9},{5... | collective-permute-start | bytes 786440 | tf_op jit(solution)/shard_map/ppermute | solution.py:269
  229.4 5.3 %collective-permute-start.46 = (f32[2,64,128]{2,1,0:T(8,128)S(1)}, f32[2,64,128]{2,1,0:T(8,128)S(1)}, u32[]{:S(2)}, u32[]{:S(2)}) collective-permute-start(f32[2,64,128]{2,1,0:T(8,128)S(1)} %bitcast.122), channel_id=1, source_target_pairs={{0,3},{1,2},{2,1},{3,0},{4,7},{5,6},{6,5},{7,4},{8,11},{9,10},{10,... | collective-permute-start | bytes 196616 | tf_op jit(solution)/shard_map/ppermute | solution.py:273
  229.7 5.0 %collective-permute-start.45 = (f32[2,64,128]{2,1,0:T(8,128)S(1)}, f32[2,64,128]{2,1,0:T(8,128)S(1)}, u32[]{:S(2)}, u32[]{:S(2)}) collective-permute-start(f32[2,64,128]{2,1,0:T(8,128)S(1)} %bitcast.121), channel_id=1, source_target_pairs={{0,2},{1,3},{2,0},{3,1},{4,6},{5,7},{6,4},{7,5},{8,10},{9,11},{10,... | collective-permute-start | bytes 196616 | tf_op jit(solution)/shard_map/ppermute | solution.py:273
  231.2 4.3 %collective-permute-start.44 = (f32[2,64,128]{2,1,0:T(8,128)S(1)}, f32[2,64,128]{2,1,0:T(8,128)S(1)}, u32[]{:S(2)}, u32[]{:S(2)}) collective-permute-start(f32[2,64,128]{2,1,0:T(8,128)S(1)} %bitcast.120), channel_id=1, source_target_pairs={{0,1},{1,0},{2,3},{3,2},{4,5},{5,4},{6,7},{7,6},{8,9},{9,8},{10,11... | collective-permute-start | bytes 196616 | tf_op jit(solution)/shard_map/ppermute | solution.py:273
  (20 other events, 29.3 us)

commit v2 on v1

v2 whole, which is shorter than its diff:
```python
import jax
import jax.numpy as jnp
from jax import lax
from jax.experimental import pallas as pl
from jax.experimental.pallas import tpu as pltpu
from jax.sharding import PartitionSpec as P


BLOCK = 128
LANES = 128
HIGH = lax.Precision.HIGH
F32 = jnp.float32
BF16 = jnp.bfloat16


def matmul(left, right):
    return jnp.dot(left, right, precision=HIGH, preferred_element_type=F32)


def matmul_left_t(left, right):
    return lax.dot_general(
        left, right, (((0,), (0,)), ((), ())), precision=HIGH, preferred_element_type=F32
    )


def select_rows(values, row_block, chosen):
    hit = jnp.any(row_block[:, None] == chosen[None, :], axis=1)
    return jnp.where(hit[:, None], values, jnp.float32(0.0))


def take(values, index, axis):
    return lax.dynamic_index_in_dim(values, index, axis, keepdims=False)


def split_two(values):
    high = values.astype(BF16)
    low = (values - high.astype(F32)).astype(BF16)
    return high, low


def product_kernel(shape, *refs):
    count, line, first_hop, last_hop, parts, rows, picks, extra, seeded = shape
    per_group = rows * count // BLOCK
    per_device = rows // BLOCK
    inputs = 3 + 2 * (last_hop - first_hop) * parts
    chosen_ref, place_ref, resident_ref = refs[:3]
    pieces = refs[3:inputs]
    seeds = refs[inputs : inputs + count] if seeded else ()
    outs = refs[inputs + len(seeds) : inputs + len(seeds) + count]
    panel_ref, resident_buf, ids_ref, panel_sem, resident_sem, extra_sem = refs[-6:]
    place, core, col = place_ref[0], place_ref[1], place_ref[2]
    width = panel_ref.shape[1]
    part = width // parts

    def parts_of(hop, other):
        first = ((hop - first_hop) * 2 + other) * parts
        return pieces[first : first + parts]

    extras = []
    if extra:
        for hop in range(first_hop, last_hop):
            source = (place + line - hop) % line
            for other in range(2):
                group = source * 2 + (core if other == 0 else 1 - core)
                for p, piece in enumerate(parts_of(hop, other)):
                    extras.append(
                        pltpu.make_async_copy(
                            piece.at[pl.ds(rows, extra), :],
                            outs[0].at[pl.ds(rows + group * extra, extra), pl.ds(p * part, part)],
                            extra_sem.at[len(extras)],
                        )
                    )

    def panel_copy(piece, inner, slot, p):
        return pltpu.make_async_copy(
            piece.at[pl.ds(inner * BLOCK, BLOCK), :],
            panel_ref.at[pl.ds(slot * BLOCK, BLOCK), pl.ds(p * part, part)],
            panel_sem.at[slot, p],
        )

    def note(i, found):
        block = chosen_ref[i]
        group = block // per_group
        inner = block % per_group
        hop = (place + line - group // 2) % line
        mine = (inner // per_device == col) & (hop >= first_hop) & (hop < last_hop)

        @pl.when(mine)
        def _():
            ids_ref[found] = group * per_device + inner % per_device
            side = hop * 2 + jnp.where(group % 2 == core, 0, 1)
            for h in range(first_hop, last_hop):
                for other in range(2):

                    @pl.when(side == h * 2 + other)
                    def _():
                        for p, piece in enumerate(parts_of(h, other)):
                            panel_copy(piece, inner % per_device, found, p).start()

        return found + mine.astype(jnp.int32)

    found = lax.fori_loop(0, picks, note, jnp.int32(0))
    ids_ref[found] = ids_ref[jnp.maximum(found - 1, 0)]
    pairs = (found + 1) // 2

    def fetch(pair, slot):
        return [
            pltpu.make_async_copy(
                resident_ref.at[pl.ds(ids_ref[2 * pair + k] * BLOCK, BLOCK), :],
                resident_buf.at[slot, pl.ds(k * BLOCK, BLOCK), :],
                resident_sem.at[slot, k],
            )
            for k in range(2)
        ]

    @pl.when(pairs > 0)
    def _():
        for copy in fetch(0, 0):
            copy.start()

    for copy in extras:
        copy.start()
    for j, out in enumerate(outs):
        out[pl.ds(0, rows), :] = seeds[j][...] if seeded else jnp.zeros((rows, width), F32)

    def step(pair, carry):
        slot = pair % 2

        @pl.when(pair + 1 < pairs)
        def _():
            for copy in fetch(pair + 1, 1 - slot):
                copy.start()

        for p in range(parts):
            panel_copy(pieces[p], 0, 2 * pair, p).wait()

        @pl.when(2 * pair + 1 < found)
        def _():
            for p in range(parts):
                panel_copy(pieces[p], 0, 2 * pair + 1, p).wait()

        first = pl.multiple_of(pair * 2 * BLOCK, BLOCK)
        both = panel_ref[pl.ds(first, 2 * BLOCK), :]
        known = lax.broadcasted_iota(jnp.int32, both.shape, 0) < (found - 2 * pair) * BLOCK
        high, low = split_two(jnp.where(known, both, jnp.float32(0.0)))
        right = jnp.concatenate([high, low, high], axis=0)
        for copy in fetch(pair, slot):
            copy.wait()
        for j in range(count):
            start = pl.multiple_of((col ^ j) * rows, LANES)
            high, low = split_two(resident_buf[slot, :, pl.ds(start, rows)])
            left = jnp.concatenate([high, high, low], axis=0)
            outs[j][pl.ds(0, rows), :] += lax.dot_general(
                left, right, (((0,), (0,)), ((), ())), preferred_element_type=F32
            )
        return carry

    lax.fori_loop(0, pairs, step, 0)
    for copy in extras:
        copy.wait()
    if extra:
        for out in outs[1:]:
            out[pl.ds(rows, 2 * line * extra), :] = outs[0][pl.ds(rows, 2 * line * extra), :]


def terms_kernel(shape, *refs):
    count, line, rows, picks, share = shape
    chosen_ref, place_ref = refs[:2]
    panels = refs[2 : 2 + count]
    products = refs[2 + count : 2 + 2 * count]
    start_ref, mine_ref, other_ref = refs[2 + 2 * count : 5 + 2 * count]
    panel_ref, product_ref, total_ref, ids_ref, sems = refs[-5:]
    row, core, col = place_ref[0], place_ref[1], place_ref[2]
    per_group = rows * count // BLOCK
    per_device = rows // BLOCK
    copies = []
    for j in range(count):
        for k, (source, target) in enumerate(((panels[j], panel_ref), (products[j], product_ref))):
            copies.append(
                pltpu.make_async_copy(source, target.at[pl.ds(j * rows, rows), :], sems.at[j, k])
            )
    for copy in copies:
        copy.start()

    def note(i, found):
        block = chosen_ref[i]
        inner = block % per_group
        mine = block // per_group == row

        @pl.when(mine)
        def _():
            ids_ref[found] = ((inner // per_device) ^ col) * per_device + inner % per_device

        return found + mine.astype(jnp.int32)

    found = lax.fori_loop(0, picks, note, jnp.int32(0))
    ids_ref[found] = ids_ref[jnp.maximum(found - 1, 0)]
    total_ref[...] = start_ref[...]
    for copy in copies:
        copy.wait()

    def step(pair, carry):
        def both(ref):
            return jnp.concatenate(
                [
                    ref[pl.ds(pl.multiple_of(ids_ref[2 * pair + k] * BLOCK, BLOCK), BLOCK), :]
                    for k in range(2)
                ],
                axis=0,
            )

        value = both(panel_ref)
        known = lax.broadcasted_iota(jnp.int32, value.shape, 0) < (found - 2 * pair) * BLOCK
        high, low = split_two(jnp.where(known, value, jnp.float32(0.0)))
        left = jnp.concatenate([high, high, low], axis=0)
        high, low = split_two(both(product_ref))
        right = jnp.concatenate([high, low, high], axis=0)
        total_ref[...] += lax.dot_general(
            left, right, (((0,), (0,)), ((), ())), preferred_element_type=F32
        )
        return carry

    lax.fori_loop(0, (found + 1) // 2, step, 0)
    for place in range(line):
        for target, side in ((mine_ref, core), (other_ref, 1 - core)):
            first = pl.multiple_of((place * 2 + side) * share, 8)
            target[place] = total_ref[pl.ds(first, share), :]


def add_terms(panels, products, start, chosen, position, line):
    count = len(panels)
    rows, width = panels[0].shape
    share = width // (2 * line)
    picks = chosen.shape[0]
    smem = pl.BlockSpec(memory_space=pltpu.SMEM)
    hbm = pl.BlockSpec(memory_space=pl.ANY)
    vmem = pl.BlockSpec(memory_space=pltpu.VMEM)
    return pl.pallas_call(
        lambda *refs: terms_kernel((count, line, rows, picks, share), *refs),
        out_shape=[jax.ShapeDtypeStruct((line, share, width), F32)] * 2,
        in_specs=[smem, smem] + [hbm] * (2 * count) + [vmem],
        out_specs=[vmem] * 2,
        scratch_shapes=[
            pltpu.VMEM((count * rows, width), F32),
            pltpu.VMEM((count * rows, width), F32),
            pltpu.VMEM((width, width), F32),
            pltpu.SMEM((picks + 2,), jnp.int32),
            pltpu.SemaphoreType.DMA((count, 2)),
        ],
        name="terms",
    )(chosen, jnp.stack(position).astype(jnp.int32), *panels, *products, start)


def in_kernel(rows):
    return rows % LANES == 0 and rows % BLOCK == 0


def fold(resident_t, hops, first_hop, last_hop, parts, chosen, position, line, col_count, extra, seeds):
    rows = resident_t.shape[1] // col_count
    width = sum(piece.shape[1] for piece in hops[0][0])
    flat = [piece for hop in hops[first_hop:last_hop] for side in hop for piece in side]
    picks = chosen.shape[0]
    smem = pl.BlockSpec(memory_space=pltpu.SMEM)
    hbm = pl.BlockSpec(memory_space=pl.ANY)
    vmem = pl.BlockSpec(memory_space=pltpu.VMEM)
    seeds = list(seeds or ())
    shape = (col_count, line, first_hop, last_hop, parts, rows, picks, extra, bool(seeds))
    inputs = 3 + len(flat)
    blocks_here = 2 * line * rows // BLOCK
    return pl.pallas_call(
        lambda *refs: product_kernel(shape, *refs),
        out_shape=[jax.ShapeDtypeStruct((rows + 2 * line * extra, width), F32)] * col_count,
        in_specs=[smem, smem, hbm] + [hbm] * len(flat) + [vmem] * len(seeds),
        out_specs=[vmem] * col_count,
        input_output_aliases={inputs + j: j for j in range(len(seeds))},
        scratch_shapes=[
            pltpu.VMEM(((blocks_here + 2) * BLOCK, width), F32),
            pltpu.VMEM((2, 2 * BLOCK, resident_t.shape[1]), F32),
            pltpu.SMEM((picks + 2,), jnp.int32),
            pltpu.SemaphoreType.DMA((blocks_here + 2, parts)),
            pltpu.SemaphoreType.DMA((2, 2)),
            pltpu.SemaphoreType.DMA((len(flat),)),
        ],
        name="fold",
    )(chosen, jnp.stack(position).astype(jnp.int32), resident_t, *flat, *seeds)


def assemble(hops, position, line, first_row, rows):
    place, core, _ = position
    width = sum(piece.shape[1] for piece in hops[0][0])
    whole = jnp.zeros((line, 2, rows, width), F32)
    for hop in range(line):
        source = (place - hop) % line
        for other in range(2):
            value = jnp.concatenate(hops[hop][other], axis=1)[first_row : first_row + rows]
            side = core if other == 0 else 1 - core
            whole = lax.dynamic_update_slice(whole, value[None, None], (source, side, 0, 0))
    return whole.reshape(-1, width)


def fold_plain(resident_t, hops, position, line, col_count):
    rows = resident_t.shape[1] // col_count
    folded = matmul_left_t(resident_t, assemble(hops, position, line, 0, rows))
    folded = folded.reshape(col_count, rows, -1)
    return [take(folded, position[2] ^ j, 0) for j in range(col_count)]


def body(*arguments):
    fused = in_kernel(arguments[1].shape[1])
    return compute(fused, *arguments)


def compute(fused, ancestor, panels, link_panels, diag_inverse, blocks):
    row_count = lax.axis_size("row")
    col_count = lax.axis_size("col")
    row_index = lax.axis_index("row")
    col_index = lax.axis_index("col")
    line = row_count // 2
    place = row_index // 2
    core = row_index % 2
    resident_t = ancestor.reshape(ancestor.shape[0] * ancestor.shape[1], ancestor.shape[2])
    supernodes, rows_here, width = panels.shape
    rows_part = width // row_count
    cols_part = width // col_count
    share_rows = rows_part // col_count
    first_row = (row_index * col_count + col_index) * rows_here
    row_block = (first_row + jnp.arange(rows_here, dtype=jnp.int32)) // BLOCK
    swap = [(i, i ^ 1) for i in range(row_count)]

    def ring(hop):
        return [(i, (i + 2 * hop) % row_count) for i in range(row_count)]

    def near(j):
        return [(i, i ^ j) for i in range(col_count)]

    masked = [select_rows(panels[s], row_block, blocks[s]) for s in range(supernodes)]
    link_own = [
        lax.dynamic_slice_in_dim(link_panels[s], col_index * share_rows, share_rows, 0)
        for s in range(supernodes - 1)
    ]

    parts = 2
    part = width // parts
    position = (place, core, col_index)
    tie = lax.optimization_barrier if fused else lambda values: values

    def streams(s):
        values = []
        for p in range(parts):
            rows = [masked[s][:, p * part : (p + 1) * part]]
            if s + 1 < supernodes:
                rows.append(link_own[s][:, p * part : (p + 1) * part])
            values.append(jnp.concatenate(rows, axis=0))
        return values

    def both(values):
        return values, [lax.ppermute(value, "row", swap) for value in values]

    def shift(values):
        return [lax.ppermute(value, "row", ring(1)) for value in values]

    near_rows = [
        [masked[s]]
        + [lax.ppermute(masked[s], "col", near(j)) for j in range(1, col_count)]
        if s > 0
        else None
        for s in range(supernodes)
    ]
    near_rows = tuple(near_rows)

    global_rows = row_index * rows_part + col_index * share_rows + jnp.arange(share_rows, dtype=jnp.int32)
    keep = jnp.arange(width, dtype=jnp.int32)[None, :] <= global_rows[:, None]
    slabs = []
    for s in range(supernodes):
        slab = lax.dynamic_slice_in_dim(diag_inverse[s], col_index * share_rows, share_rows, 0)
        slab = jnp.where(keep, slab, jnp.float32(0.0))
        slabs.append(matmul_left_t(slab, slab))

    folds, products = [], []
    ahead = streams(0)
    for s in range(supernodes):
        last = s + 1 == supernodes
        extra = 0 if last else share_rows
        now = ahead
        hops = [both(now)]
        for hop in range(1, line):
            if hop > 1:
                now, hops[hop - 2] = tie((now, hops[hop - 2]))
            if hop == line - 1 and s == 0:
                now, slabs = tie((now, slabs))
            now = shift(now)
            if hop == 1 and s > 0:
                now, folds[s - 1] = tie((now, folds[s - 1]))
            if hop == line - 1 and last:
                hops, near_rows = tie((hops, near_rows))
                if fused:
                    made = fold(
                        resident_t, hops, 0, hop, parts, blocks[s], position, line, col_count, 0, None
                    )
                    now, made = tie((now, made))
            hops.append(both(now))
            if hop == line - 2 and not last:
                ahead, _ = tie((streams(s + 1), now))
        if fused:
            begin, seeds = (line - 1, made) if last and line > 1 else (0, None)
            made = fold(
                resident_t, hops, begin, line, parts, blocks[s], position, line, col_count, extra, seeds
            )
        else:
            made = fold_plain(resident_t, hops, position, line, col_count)
            if extra:
                tail = assemble(hops, position, line, rows_here, extra)
                made = [jnp.concatenate([value, tail], axis=0) for value in made]
        folds.append(made)
        products.append(
            [made[0]]
            + [lax.ppermute(made[j], "col", near(j)) for j in range(1, col_count)]
        )
    products[0], folds[-1] = tie((products[0], folds[-1]))

    def link_whole(s):
        whole = jnp.zeros((row_count, col_count, share_rows, width), F32)
        for j in range(col_count):
            value = products[s][j][rows_here:].reshape(row_count, 1, share_rows, width)
            whole = lax.dynamic_update_slice(whole, value, (0, col_index ^ j, 0, 0))
        return whole.reshape(width, width)

    links = [link_whole(s) for s in range(supernodes - 1)]

    def reduce_line(mine, theirs):
        view = mine + lax.ppermute(theirs, "row", swap)
        total = take(view, place, 0)
        for hop in range(1, line):
            target = (place + hop) % line
            total = total + lax.ppermute(take(view, target, 0), "row", ring(hop))
        return total

    def reduce_near(totals):
        view = totals.reshape(totals.shape[0], rows_part, col_count, cols_part)
        total = take(view, col_index, 2)
        for j in range(1, col_count):
            total = total + lax.ppermute(take(view, col_index ^ j, 2), "col", near(j))
        return total

    def by_core(partial):
        view = partial.reshape(line, 2, rows_part, width)
        return take(view, core, 1), take(view, 1 - core, 1)

    col_list, partials, totals = [], [], []
    for s in range(supernodes):
        partial = slabs[s]
        product = products[s][0]
        for j in range(1, col_count):
            product = product + products[s][j]
        product = product[:rows_here]
        if s == 0:
            cols_now = -product
            partial = partial - matmul_left_t(masked[s], cols_now)
        else:
            link = links[s - 1]
            carried = matmul(col_list[-1], link)
            cols_now = -(product + carried)
            partial = partial + matmul_left_t(carried, masked[s])
            partial = partial + matmul_left_t(masked[s], carried)
            partial = partial + matmul_left_t(link, matmul(partials[-1], link))
            if not fused:
                for j in range(col_count):
                    partial = partial + matmul_left_t(near_rows[s][j], folds[s][j])
        col_list.append(cols_now)
        partials.append(partial)
        if s > 0 and fused:
            sides = add_terms(
                near_rows[s], folds[s], partial, blocks[s], (row_index, core, col_index), line
            )
        else:
            sides = by_core(partial)
        totals.append(reduce_line(*sides))
    return (jnp.stack(col_list), reduce_near(jnp.stack(totals)))


def solution(mesh):
    placed = (
        P(None, "col", "row"),
        P(None, ("row", "col"), None),
        P(None, "row", None),
        P(None, "row", None),
        P(),
    )
    return jax.shard_map(
        body,
        mesh=mesh,
        in_specs=placed,
        out_specs=(P(None, ("row", "col"), None), P(None, "row", "col")),
        check_vma=False,
    )
```

time: 238 us -> 252 us (1.059)
  Pallas kernels: 29.6 us -> 50.8 us
  waiting for transfers between devices: 115 us -> 134 us
  starting transfers between devices: 42.3 us -> 30.9 us
  matrix products: 19.2 us -> 10.3 us
  local copies, waits for them, and re-layouts: 18.1 us -> 11 us
    ppermute x12, waiting for transfers between devices: 56.9 us -> 83.1 us  [shift(): return [lax.ppermute(value, 'row', ring(1)) for value in values]]
    pallas_call x2 -> x4, Pallas kernels: 29.6 us -> 50.8 us  [the longest x3 44.3 us: fold(): pl.pallas_call(lambda *refs: product_kernel(shape, *refs), out_shape=[jax...]
    ppermute x19 -> x20, starting transfers between devices: 27.2 us -> 17.8 us  [the longest x6 6.24 us: compute(): lax.ppermute(made[j], 'col', near(j))]
    dot_general x10 -> x6, matrix products: 17.3 us -> 8.44 us  [matmul_left_t(): lax.dot_general(left, right, (((0,), (0,)), ((), ())), precision=HIGH, pr...]
    ppermute x19 -> x20, waiting for transfers between devices: 57.7 us -> 49.9 us  [the longest x6 19.6 us: reduce_line(): total = total + lax.ppermute(take(view, target, 0), 'row', ring(hop))]
    slice x18 -> x6, local copies, waits for them, and re-layouts: 8.18 us -> 4.81 us  [the longest x5 3.83 us: link_whole(): value = products[s][j][rows_here:].reshape(row_count, 1, share_rows, width)]
    dynamic_update_slice x4, local copies, waits for them, and re-layouts: 2.95 us -> 0.1 us  [link_whole(): whole = lax.dynamic_update_slice(whole, value, (0, col_index ^ j, 0, 0))]
  transfers between devices with their start and end apart: 47 -> 48, of which waited for: 15 -> 20; matrix products, arithmetic and copies ran while one was open for 13% -> 4% of each run, Pallas kernels for 7% -> 18%
where the time goes in v2:
time: 252 us; the launch traced here: 249 us
  waiting for transfers between devices  134 us (53%)
  Pallas kernels  50.8 us (20%)
  starting transfers between devices  30.9 us (12%)
  local copies, waits for them, and re-layouts  11 us (4%)
  other arithmetic  10.8 us (4%)
  matrix products  10.3 us (4%)
    ppermute x12, waiting for transfers between devices, shift(): return [lax.ppermute(value, 'row', ring(1)) for value in values]  83.1 us
    pallas_call x3, Pallas kernels, fold(): pl.pallas_call(lambda *refs: product_kernel(shape, *refs), out_shape=[jax...  44.3 us
    ppermute x6, waiting for transfers between devices, reduce_line(): total = total + lax.ppermute(take(view, target, 0), 'row', ring(hop))  19.6 us
    ppermute x3, waiting for transfers between devices, reduce_near(): total = total + lax.ppermute(take(view, col_index ^ j, 2), 'col', near(j))  11.9 us
    ppermute x12, starting transfers between devices, shift(): return [lax.ppermute(value, 'row', ring(1)) for value in values]  10.3 us
    ppermute x3, waiting for transfers between devices, compute(): lax.ppermute(masked[s], 'col', near(j))  9.72 us
    ppermute x6, waiting for transfers between devices, compute(): lax.ppermute(made[j], 'col', near(j))  8.66 us
    dot_general x6, matrix products, matmul_left_t(): lax.dot_general(left, right, (((0,), (0,)), ((), ())), precision=HIGH, pr...  8.44 us
  transfers between devices with their start and end apart: 48, of which 20 were waited for; matrix products, arithmetic and copies ran while one was open for 4% of the time, Pallas kernels for 18%

profile of v2, /device:TPU:0, one launch (start us, length us, event | category | flops | bytes accessed | tf_op | source)
XLA Modules:
  0.0 249.5 jit_solution(12244458348969249245)
XLA Ops:
  0.7 0.8 slice_bitcast_fusion
  1.5 1.6 bitcast_select_fusion
  3.3 3.1 %collective-permute-start.1 = (f32[400,256]{1,0:T(8,128)S(1)}, f32[400,256]{1,0:T(8,128)S(1)}, u32[]{:S(2)}, u32[]{:S(2)}) collective-permute-start(f32[400,256]{1,0:T(8,128)S(1)} %pad_maximum_fusion.2.refs_4_), channel_id=1, source_target_pairs={{0,8},{4,12},{8,16},{12,20},{16,24},{20,28},{24,0},{28,4},{1,9},{5... | collective-permute-start | bytes 1228808 | tf_op jit(solution)/shard_map/ppermute | solution.py:360
  6.4 1.6 collective-permute-start
  8.6 1.0 fusion.26
  9.6 9.2 %collective-permute-done.1.refs_8_ = f32[400,256]{1,0:T(8,128)S(1)} collective-permute-done((f32[400,256]{1,0:T(8,128)S(1)}, f32[400,256]{1,0:T(8,128)S(1)}, u32[]{:S(2)}, u32[]{:S(2)}) %collective-permute-start.1) | collective-permute-done | bytes 409632 | tf_op jit(solution)/shard_map/ppermute | solution.py:360
  18.7 8.0 %collective-permute-done.refs_7_ = f32[400,256]{1,0:T(8,128)} collective-permute-done((f32[400,256]{1,0:T(8,128)S(1)}, f32[400,256]{1,0:T(8,128)}, u32[]{:S(2)}, u32[]{:S(2)}) %collective-permute-start) | collective-permute-done | bytes 409632 | tf_op jit(solution)/shard_map/ppermute | solution.py:360
  26.8 1.3 collective-permute-start.5
  28.6 1.7 fusion.5
  30.2 1.7 fusion.7
  31.9 9.2 %collective-permute-done.4.refs_11_ = f32[400,256]{1,0:T(8,128)S(1)} collective-permute-done((f32[400,256]{1,0:T(8,128)}, f32[400,256]{1,0:T(8,128)S(1)}, u32[]{:S(2)}, u32[]{:S(2)}) %collective-permute-start.4) | collective-permute-done | bytes 409632 | tf_op jit(solution)/shard_map/ppermute | solution.py:360
  41.1 7.1 %collective-permute-done.5.refs_12_ = f32[400,256]{1,0:T(8,128)S(1)} collective-permute-done((f32[400,256]{1,0:T(8,128)S(1)}, f32[400,256]{1,0:T(8,128)S(1)}, u32[]{:S(2)}, u32[]{:S(2)}) %collective-permute-start.5) | collective-permute-done | bytes 409632 | tf_op jit(solution)/shard_map/ppermute | solution.py:360
  48.3 0.7 copy-done.15
  49.4 3.9 %collective-permute-start.18 = (f32[384,256]{1,0:T(8,128)S(1)}, f32[384,256]{1,0:T(8,128)S(1)}, u32[]{:S(2)}, u32[]{:S(2)}) collective-permute-start(f32[384,256]{1,0:T(8,128)S(1)} %get-tuple-element.113.refs_4_), channel_id=1, source_target_pairs={{0,8},{4,12},{8,16},{12,20},{16,24},{20,28},{24,0},{28,4},{1,9},{5... | collective-permute-start | bytes 1179656 | tf_op jit(solution)/shard_map/ppermute | solution.py:360
  53.4 17.5 %collective-permute-done.17.refs_7_ = f32[384,256]{1,0:T(8,128)} collective-permute-done((f32[384,256]{1,0:T(8,128)S(1)}, f32[384,256]{1,0:T(8,128)}, u32[]{:S(2)}, u32[]{:S(2)}) %collective-permute-start.17) | collective-permute-done | bytes 393248 | tf_op jit(solution)/shard_map/ppermute | solution.py:360
  71.4 8.2 %collective-permute-done.11.refs_16_ = f32[400,256]{1,0:T(8,128)S(1)} collective-permute-done((f32[400,256]{1,0:T(8,128)S(1)}, f32[400,256]{1,0:T(8,128)S(1)}, u32[]{:S(2)}, u32[]{:S(2)}) %collective-permute-start.11) | collective-permute-done | bytes 409632 | tf_op jit(solution)/shard_map/ppermute | solution.py:360
  79.6 5.9 %collective-permute-done.18.refs_8_ = f32[384,256]{1,0:T(8,128)S(1)} collective-permute-done((f32[384,256]{1,0:T(8,128)S(1)}, f32[384,256]{1,0:T(8,128)S(1)}, u32[]{:S(2)}, u32[]{:S(2)}) %collective-permute-start.18) | collective-permute-done | bytes 393248 | tf_op jit(solution)/shard_map/ppermute | solution.py:360
  85.5 1.1 collective-permute-start.29
  86.5 1.5 collective-permute-start.30
  89.0 0.8 copy-done.22
  89.7 0.9 collective-permute-start.31
  91.2 18.7 %fold.3 = (f32[512,512]{1,0:T(8,128)}, f32[512,512]{1,0:T(8,128)}, f32[512,512]{1,0:T(8,128)}, f32[512,512]{1,0:T(8,128)}) custom-call(s32[48]{0:T(128)} %copy-done.32, s32[3]{0:T(128)} %add_add_fusion.1.refs_1_, f32[3072,1536]{1,0:T(8,128)} %bitcast.82, f32[400,256]{1,0:T(8,128)} %copy-done.7, f32[400,256]{1,0:T(8,128)} %copy-done.6, ...), custom_call_target="tpu_custom_call" | custom-call | tf_op jit(solution)/shard_map/fold/pallas_call | solution.py:270
  110.3 9.7 %collective-permute-done.30.refs_4_ = f32[384,512]{1,0:T(8,128)} collective-permute-done((f32[384,512]{1,0:T(8,128)S(1)}, f32[384,512]{1,0:T(8,128)}, u32[]{:S(2)}, u32[]{:S(2)}) %collective-permute-start.30) | collective-permute-done | bytes 786464 | tf_op jit(solution)/shard_map/ppermute | solution.py:364
  120.0 4.0 %collective-permute-done.21.refs_11_ = f32[384,256]{1,0:T(8,128)S(1)} collective-permute-done((f32[384,256]{1,0:T(8,128)}, f32[384,256]{1,0:T(8,128)S(1)}, u32[]{:S(2)}, u32[]{:S(2)}) %collective-permute-start.21) | collective-permute-done | bytes 393248 | tf_op jit(solution)/shard_map/ppermute | solution.py:360
  124.0 7.7 %collective-permute-done.22.refs_12_ = f32[384,256]{1,0:T(8,128)} collective-permute-done((f32[384,256]{1,0:T(8,128)}, f32[384,256]{1,0:T(8,128)}, u32[]{:S(2)}, u32[]{:S(2)}) %collective-permute-start.22) | collective-permute-done | bytes 393248 | tf_op jit(solution)/shard_map/ppermute | solution.py:360
  131.7 0.8 collective-permute-start.15
  132.5 2.7 %collective-permute-start.16 = (f32[512,512]{1,0:T(8,128)}, f32[512,512]{1,0:T(8,128)}, u32[]{:S(2)}, u32[]{:S(2)}) collective-permute-start(f32[512,512]{1,0:T(8,128)} %get-tuple-element.95), channel_id=1, source_target_pairs={{0,3},{1,2},{2,1},{3,0},{4,7},{5,6},{6,5},{7,4},{8,11},{9,10},{10,... | collective-permute-start | bytes 3145736 | tf_op jit(solution)/shard_map/ppermute | solution.py:417
  135.3 0.7 copy-done.29
  136.0 0.7 copy-done.30
  136.7 13.1 %fold.4 = (f32[384,512]{1,0:T(8,128)}, f32[384,512]{1,0:T(8,128)}, f32[384,512]{1,0:T(8,128)}, f32[384,512]{1,0:T(8,128)}) custom-call(s32[48]{0:T(128)} %copy-done.31, s32[3]{0:T(128)} %add_add_fusion.1.refs_1_, f32[3072,1536]{1,0:T(8,128)} %bitcast.83, f32[384,256]{1,0:T(8,128)} %copy-done.9, f32[384,256]{1,0:T(8,128)} %copy-done.8, ...), custom_call_target="tpu_custom_call" | custom-call | tf_op jit(solution)/shard_map/fold/pallas_call | solution.py:270
  149.8 6.4 %collective-permute-done.26.refs_4_ = f32[384,256]{1,0:T(8,128)} collective-permute-done((f32[384,256]{1,0:T(8,128)}, f32[384,256]{1,0:T(8,128)}, u32[]{:S(2)}, u32[]{:S(2)}) %collective-permute-start.26) | collective-permute-done | bytes 393248 | tf_op jit(solution)/shard_map/ppermute | solution.py:360
  158.0 0.7 collective-permute-done.33.refs_6_
  158.8 12.5 %fold.5 = (f32[384,512]{1,0:T(8,128)}, f32[384,512]{1,0:T(8,128)}, f32[384,512]{1,0:T(8,128)}, f32[384,512]{1,0:T(8,128)}) custom-call(s32[48]{0:T(128)} %copy-done.31, s32[3]{0:T(128)} %add_add_fusion.1.refs_1_, f32[3072,1536]{1,0:T(8,128)} %bitcast.84, ...), custom_call_target="tpu_custom_call", output_to_operand_aliasing={{0}: (7, {}), {1}: (8, {}), {2}: (9, {}), {3}: (10, {})} | custom-call | tf_op jit(solution)/shard_map/fold/pallas_call | solution.py:270
  171.4 8.6 %collective-permute-done.15 = f32[512,512]{1,0:T(8,128)S(1)} collective-permute-done((f32[512,512]{1,0:T(8,128)}, f32[512,512]{1,0:T(8,128)S(1)}, u32[]{:S(2)}, u32[]{:S(2)}) %collective-permute-start.15) | collective-permute-done | bytes 1048608 | tf_op jit(solution)/shard_map/ppermute | solution.py:417
  180.0 1.1 slice.68
  181.2 1.0 slice.69
  182.2 1.8 fusion
  184.0 1.0 slice.71
  185.0 1.1 convolution_subtract_fusion
  186.2 0.7 slice-done
  187.0 0.8 fusion.28
  187.9 1.0 fusion.29
  189.1 1.0 convolution_add_fusion.1
  190.1 1.0 convolution_add_fusion
  191.2 2.0 convolution_add_fusion.2.refs_10_
  193.1 6.4 %terms.1 = (f32[4,64,512]{2,1,0:T(8,128)}, f32[4,64,512]{2,1,0:T(8,128)}) custom-call(s32[48]{0:T(128)} %copy-done.31, s32[3]{0:T(128)} %add_add_fusion.2.refs_1_, f32[384,512]{1,0:T(8,128)} %copy-done.2, f32[384,512]{1,0:T(8,128)} %collective-permute-done.29.refs_3_, f32[384,512]{1,0:T(8,128)} %collective-permute-done.30.refs_4_, ...), custom_call_target="tpu_custom_call" | custom-call | tf_op jit(solution)/shard_map/terms/pallas_call | solution.py:238
  200.0 0.8 dynamic-slice_bitcast_fusion
  201.0 1.7 collective-permute-start.34
  203.0 1.1 add.208
  204.2 1.4 collective-permute-start.43
  205.6 2.4 collective-permute-start.44
  208.0 1.1 bitcast_add_fusion
  209.2 3.2 %collective-permute-done.42 = f32[64,512]{1,0:T(8,128)S(1)} collective-permute-done((f32[64,512]{1,0:T(8,128)S(1)}, f32[64,512]{1,0:T(8,128)S(1)}, u32[]{:S(2)}, u32[]{:S(2)}) %collective-permute-start.42) | collective-permute-done | bytes 131104 | tf_op jit(solution)/shard_map/ppermute | solution.py:435
  212.4 8.6 %collective-permute-done.43 = f32[64,512]{1,0:T(8,128)S(1)} collective-permute-done((f32[64,512]{1,0:T(8,128)S(1)}, f32[64,512]{1,0:T(8,128)S(1)}, u32[]{:S(2)}, u32[]{:S(2)}) %collective-permute-start.43) | collective-permute-done | bytes 131104 | tf_op jit(solution)/shard_map/ppermute | solution.py:435
  221.1 0.8 collective-permute-start.36
  221.9 6.2 %collective-permute-done.39 = f32[64,512]{1,0:T(8,128)S(1)} collective-permute-done((f32[64,512]{1,0:T(8,128)S(1)}, f32[64,512]{1,0:T(8,128)S(1)}, u32[]{:S(2)}, u32[]{:S(2)}) %collective-permute-start.39) | collective-permute-done | bytes 131104 | tf_op jit(solution)/shard_map/ppermute | solution.py:435
  228.1 1.6 collective-permute-done.40
  230.2 1.5 collective-permute-start.45
  231.7 0.7 collective-permute-start.46
  232.4 8.1 %collective-permute-done.45 = f32[2,64,128]{2,1,0:T(8,128)S(1)} collective-permute-done((f32[2,64,128]{2,1,0:T(8,128)S(1)}, f32[2,64,128]{2,1,0:T(8,128)S(1)}, u32[]{:S(2)}, u32[]{:S(2)}) %collective-permute-start.45) | collective-permute-done | bytes 65568 | tf_op jit(solution)/shard_map/ppermute | solution.py:442
  240.5 1.4 collective-permute-start.47
  241.9 3.8 %collective-permute-done.47 = f32[2,64,128]{2,1,0:T(8,128)S(1)} collective-permute-done((f32[2,64,128]{2,1,0:T(8,128)S(1)}, f32[2,64,128]{2,1,0:T(8,128)S(1)}, u32[]{:S(2)}, u32[]{:S(2)}) %collective-permute-start.47) | collective-permute-done | bytes 65568 | tf_op jit(solution)/shard_map/ppermute | solution.py:442
  246.3 1.8 negate_bitcast_fusion
  248.2 1.3 pad_maximum_fusion
  (150 shorter events, 8.6 us)
Async XLA Ops:
  3.1 187.0 %copy-start.2 = (f32[384,512]{1,0:T(8,128)}, f32[384,512]{1,0:T(8,128)S(1)}, u32[]{:S(2)}) copy-start(f32[384,512]{1,0:T(8,128)S(1)} %get-tuple-element.143.refs_2_) | copy-start | bytes 2359300
  3.3 28.7 %copy-start.6 = (f32[400,256]{1,0:T(8,128)}, f32[400,256]{1,0:T(8,128)S(1)}, u32[]{:S(2)}) copy-start(f32[400,256]{1,0:T(8,128)S(1)} %pad_maximum_fusion.2.refs_4_) | copy-start | bytes 1228804
  3.3 15.4 %collective-permute-start.1 = (f32[400,256]{1,0:T(8,128)S(1)}, f32[400,256]{1,0:T(8,128)S(1)}, u32[]{:S(2)}, u32[]{:S(2)}) collective-permute-start(f32[400,256]{1,0:T(8,128)S(1)} %pad_maximum_fusion.2.refs_4_), channel_id=1, source_target_pairs={{0,8},{4,12},{8,16},{12,20},{16,24},{20,28},{24,0},{28,4},{1,9},{5... | collective-permute-start | bytes 1228808 | tf_op jit(solution)/shard_map/ppermute | solution.py:360
  6.4 42.8 %copy-start.7 = (f32[400,256]{1,0:T(8,128)}, f32[400,256]{1,0:T(8,128)S(1)}, u32[]{:S(2)}) copy-start(f32[400,256]{1,0:T(8,128)S(1)} %pad_maximum_fusion.1.refs_3_) | copy-start | bytes 1228804
  6.4 20.3 %collective-permute-start = (f32[400,256]{1,0:T(8,128)S(1)}, f32[400,256]{1,0:T(8,128)}, u32[]{:S(2)}, u32[]{:S(2)}) collective-permute-start(f32[400,256]{1,0:T(8,128)S(1)} %pad_maximum_fusion.1.refs_3_), channel_id=1, source_target_pairs={{0,8},{4,12},{8,16},{12,20},{16,24},{20,28},{24,0},{28,4},{1,9},{5... | collective-permute-start | bytes 1228808 | tf_op jit(solution)/shard_map/ppermute | solution.py:360
  8.1 18.7 %collective-permute-start.3 = (f32[400,256]{1,0:T(8,128)S(1)}, f32[400,256]{1,0:T(8,128)}, u32[]{:S(2)}, u32[]{:S(2)}) collective-permute-start(f32[400,256]{1,0:T(8,128)S(1)} %pad_maximum_fusion.2.refs_4_), channel_id=1, source_target_pairs={{0,4},{4,0},{8,12},{12,8},{16,20},{20,16},{24,28},{28,24},{1,5},{5... | collective-permute-start | bytes 1228808 | tf_op jit(solution)/shard_map/ppermute | solution.py:357
  8.1 18.7 %collective-permute-start.2 = (f32[400,256]{1,0:T(8,128)S(1)}, f32[400,256]{1,0:T(8,128)}, u32[]{:S(2)}, u32[]{:S(2)}) collective-permute-start(f32[400,256]{1,0:T(8,128)S(1)} %pad_maximum_fusion.1.refs_3_), channel_id=1, source_target_pairs={{0,4},{4,0},{8,12},{12,8},{16,20},{20,16},{24,28},{28,24},{1,5},{5... | collective-permute-start | bytes 1228808 | tf_op jit(solution)/shard_map/ppermute | solution.py:357
  18.7 30.5 %copy-start.12 = (f32[400,256]{1,0:T(8,128)}, f32[400,256]{1,0:T(8,128)S(1)}, u32[]{:S(2)}) copy-start(f32[400,256]{1,0:T(8,128)S(1)} %collective-permute-done.1.refs_8_) | copy-start | bytes 1228804
  26.8 14.3 %collective-permute-start.4 = (f32[400,256]{1,0:T(8,128)}, f32[400,256]{1,0:T(8,128)S(1)}, u32[]{:S(2)}, u32[]{:S(2)}) collective-permute-start(f32[400,256]{1,0:T(8,128)} %collective-permute-done.refs_7_), channel_id=1, source_target_pairs={{0,8},{4,12},{8,16},{12,20},{16,24},{20,28},{24,0},{28,4},{1,9},{5... | collective-permute-start | bytes 1228808 | tf_op jit(solution)/shard_map/ppermute | solution.py:360
  26.8 21.4 %collective-permute-start.5 = (f32[400,256]{1,0:T(8,128)S(1)}, f32[400,256]{1,0:T(8,128)S(1)}, u32[]{:S(2)}, u32[]{:S(2)}) collective-permute-start(f32[400,256]{1,0:T(8,128)S(1)} %collective-permute-done.1.refs_8_), channel_id=1, source_target_pairs={{0,8},{4,12},{8,16},{12,20},{16,24},{20,28},{24,0},{28,4},{1,9},{5... | collective-permute-start | bytes 1228808 | tf_op jit(solution)/shard_map/ppermute | solution.py:360
  28.1 20.1 %collective-permute-start.7 = (f32[400,256]{1,0:T(8,128)S(1)}, f32[400,256]{1,0:T(8,128)S(1)}, u32[]{:S(2)}, u32[]{:S(2)}) collective-permute-start(f32[400,256]{1,0:T(8,128)S(1)} %collective-permute-done.1.refs_8_), channel_id=1, source_target_pairs={{0,4},{4,0},{8,12},{12,8},{16,20},{20,16},{24,28},{28,24},{1,5},{5... | collective-permute-start | bytes 1228808 | tf_op jit(solution)/shard_map/ppermute | solution.py:357
  28.1 20.1 %collective-permute-start.6 = (f32[400,256]{1,0:T(8,128)}, f32[400,256]{1,0:T(8,128)S(1)}, u32[]{:S(2)}, u32[]{:S(2)}) collective-permute-start(f32[400,256]{1,0:T(8,128)} %collective-permute-done.refs_7_), channel_id=1, source_target_pairs={{0,4},{4,0},{8,12},{12,8},{16,20},{20,16},{24,28},{28,24},{1,5},{5... | collective-permute-start | bytes 1228808 | tf_op jit(solution)/shard_map/ppermute | solution.py:357
  41.1 47.5 %copy-start.13 = (f32[400,256]{1,0:T(8,128)}, f32[400,256]{1,0:T(8,128)S(1)}, u32[]{:S(2)}) copy-start(f32[400,256]{1,0:T(8,128)S(1)} %collective-permute-done.4.refs_11_) | copy-start | bytes 1228804
  48.2 40.4 %copy-start.14 = (f32[400,256]{1,0:T(8,128)}, f32[400,256]{1,0:T(8,128)S(1)}, u32[]{:S(2)}) copy-start(f32[400,256]{1,0:T(8,128)S(1)} %collective-permute-done.5.refs_12_) | copy-start | bytes 1228804
  48.2 22.7 %collective-permute-start.10 = (f32[400,256]{1,0:T(8,128)S(1)}, f32[400,256]{1,0:T(8,128)S(1)}, u32[]{:S(2)}, u32[]{:S(2)}) collective-permute-start(f32[400,256]{1,0:T(8,128)S(1)} %collective-permute-done.4.refs_11_), channel_id=1, source_target_pairs={{0,8},{4,12},{8,16},{12,20},{16,24},{20,28},{24,0},{28,4},{1,9},{5... | collective-permute-start | bytes 1228808 | tf_op jit(solution)/shard_map/ppermute | solution.py:360
  49.2 60.7 %copy-start.8 = (f32[384,256]{1,0:T(8,128)}, f32[384,256]{1,0:T(8,128)S(1)}, u32[]{:S(2)}) copy-start(f32[384,256]{1,0:T(8,128)S(1)} %get-tuple-element.113.refs_4_) | copy-start | bytes 1179652
  49.2 60.7 %copy-start.9 = (f32[384,256]{1,0:T(8,128)}, f32[384,256]{1,0:T(8,128)S(1)}, u32[]{:S(2)}) copy-start(f32[384,256]{1,0:T(8,128)S(1)} %get-tuple-element.112.refs_3_) | copy-start | bytes 1179652
  49.2 21.7 %collective-permute-start.17 = (f32[384,256]{1,0:T(8,128)S(1)}, f32[384,256]{1,0:T(8,128)}, u32[]{:S(2)}, u32[]{:S(2)}) collective-permute-start(f32[384,256]{1,0:T(8,128)S(1)} %get-tuple-element.112.refs_3_), channel_id=1, source_target_pairs={{0,8},{4,12},{8,16},{12,20},{16,24},{20,28},{24,0},{28,4},{1,9},{5... | collective-permute-start | bytes 1179656 | tf_op jit(solution)/shard_map/ppermute | solution.py:360
  49.3 30.3 %collective-permute-start.11 = (f32[400,256]{1,0:T(8,128)S(1)}, f32[400,256]{1,0:T(8,128)S(1)}, u32[]{:S(2)}, u32[]{:S(2)}) collective-permute-start(f32[400,256]{1,0:T(8,128)S(1)} %collective-permute-done.5.refs_12_), channel_id=1, source_target_pairs={{0,8},{4,12},{8,16},{12,20},{16,24},{20,28},{24,0},{28,4},{1,9},{5... | collective-permute-start | bytes 1228808 | tf_op jit(solution)/shard_map/ppermute | solution.py:360
  49.4 37.2 %collective-permute-start.8 = (f32[400,256]{1,0:T(8,128)S(1)}, f32[400,256]{1,0:T(8,128)S(1)}, u32[]{:S(2)}, u32[]{:S(2)}) collective-permute-start(f32[400,256]{1,0:T(8,128)S(1)} %collective-permute-done.4.refs_11_), channel_id=1, source_target_pairs={{0,4},{4,0},{8,12},{12,8},{16,20},{20,16},{24,28},{28,24},{1,5},{5... | collective-permute-start | bytes 1228808 | tf_op jit(solution)/shard_map/ppermute | solution.py:357
  49.4 36.0 %collective-permute-start.18 = (f32[384,256]{1,0:T(8,128)S(1)}, f32[384,256]{1,0:T(8,128)S(1)}, u32[]{:S(2)}, u32[]{:S(2)}) collective-permute-start(f32[384,256]{1,0:T(8,128)S(1)} %get-tuple-element.113.refs_4_), channel_id=1, source_target_pairs={{0,8},{4,12},{8,16},{12,20},{16,24},{20,28},{24,0},{28,4},{1,9},{5... | collective-permute-start | bytes 1179656 | tf_op jit(solution)/shard_map/ppermute | solution.py:360
  70.9 17.1 %collective-permute-start.9 = (f32[400,256]{1,0:T(8,128)S(1)}, f32[400,256]{1,0:T(8,128)S(1)}, u32[]{:S(2)}, u32[]{:S(2)}) collective-permute-start(f32[400,256]{1,0:T(8,128)S(1)} %collective-permute-done.5.refs_12_), channel_id=1, source_target_pairs={{0,4},{4,0},{8,12},{12,8},{16,20},{20,16},{24,28},{28,24},{1,5},{5... | collective-permute-start | bytes 1228808 | tf_op jit(solution)/shard_map/ppermute | solution.py:357
  70.9 17.6 %copy-start.17 = (f32[400,256]{1,0:T(8,128)}, f32[400,256]{1,0:T(8,128)S(1)}, u32[]{:S(2)}) copy-start(f32[400,256]{1,0:T(8,128)S(1)} %collective-permute-done.10.refs_15_) | copy-start | bytes 1228804
  70.9 17.1 %collective-permute-start.12 = (f32[400,256]{1,0:T(8,128)S(1)}, f32[400,256]{1,0:T(8,128)S(1)}, u32[]{:S(2)}, u32[]{:S(2)}) collective-permute-start(f32[400,256]{1,0:T(8,128)S(1)} %collective-permute-done.10.refs_15_), channel_id=1, source_target_pairs={{0,4},{4,0},{8,12},{12,8},{16,20},{20,16},{24,28},{28,24},{1,5},{5... | collective-permute-start | bytes 1228808 | tf_op jit(solution)/shard_map/ppermute | solution.py:357
  79.6 11.6 %copy-start.18 = (f32[400,256]{1,0:T(8,128)}, f32[400,256]{1,0:T(8,128)S(1)}, u32[]{:S(2)}) copy-start(f32[400,256]{1,0:T(8,128)S(1)} %collective-permute-done.11.refs_16_) | copy-start | bytes 1228804
  79.6 9.0 %collective-permute-start.13 = (f32[400,256]{1,0:T(8,128)S(1)}, f32[400,256]{1,0:T(8,128)S(1)}, u32[]{:S(2)}, u32[]{:S(2)}) collective-permute-start(f32[400,256]{1,0:T(8,128)S(1)} %collective-permute-done.11.refs_16_), channel_id=1, source_target_pairs={{0,4},{4,0},{8,12},{12,8},{16,20},{20,16},{24,28},{28,24},{1,5},{5... | collective-permute-start | bytes 1228808 | tf_op jit(solution)/shard_map/ppermute | solution.py:357
  85.5 24.6 %collective-permute-start.29 = (f32[384,512]{1,0:T(8,128)S(1)}, f32[384,512]{1,0:T(8,128)}, u32[]{:S(2)}, u32[]{:S(2)}) collective-permute-start(f32[384,512]{1,0:T(8,128)S(1)} %get-tuple-element.143.refs_2_), channel_id=1, source_target_pairs={{0,1},{1,0},{2,3},{3,2},{4,5},{5,4},{6,7},{7,6},{8,9},{9,8},{10,11... | collective-permute-start | bytes 2359304 | tf_op jit(solution)/shard_map/ppermute | solution.py:364
  86.5 4.7 %copy-start.19 = (f32[400,256]{1,0:T(8,128)}, f32[400,256]{1,0:T(8,128)S(1)}, u32[]{:S(2)}) copy-start(f32[400,256]{1,0:T(8,128)S(1)} %collective-permute-done.8.refs_13_) | copy-start | bytes 1228804
  86.5 33.5 %collective-permute-start.30 = (f32[384,512]{1,0:T(8,128)S(1)}, f32[384,512]{1,0:T(8,128)}, u32[]{:S(2)}, u32[]{:S(2)}) collective-permute-start(f32[384,512]{1,0:T(8,128)S(1)} %get-tuple-element.143.refs_2_), channel_id=1, source_target_pairs={{0,2},{1,3},{2,0},{3,1},{4,6},{5,7},{6,4},{7,5},{8,10},{9,11},{10,... | collective-permute-start | bytes 2359304 | tf_op jit(solution)/shard_map/ppermute | solution.py:364
  88.1 21.9 %collective-permute-start.19 = (f32[384,256]{1,0:T(8,128)S(1)}, f32[384,256]{1,0:T(8,128)}, u32[]{:S(2)}, u32[]{:S(2)}) collective-permute-start(f32[384,256]{1,0:T(8,128)S(1)} %get-tuple-element.112.refs_3_), channel_id=1, source_target_pairs={{0,4},{4,0},{8,12},{12,8},{16,20},{20,16},{24,28},{28,24},{1,5},{5... | collective-permute-start | bytes 1179656 | tf_op jit(solution)/shard_map/ppermute | solution.py:357
  88.1 21.9 %collective-permute-start.20 = (f32[384,256]{1,0:T(8,128)S(1)}, f32[384,256]{1,0:T(8,128)}, u32[]{:S(2)}, u32[]{:S(2)}) collective-permute-start(f32[384,256]{1,0:T(8,128)S(1)} %get-tuple-element.113.refs_4_), channel_id=1, source_target_pairs={{0,4},{4,0},{8,12},{12,8},{16,20},{20,16},{24,28},{28,24},{1,5},{5... | collective-permute-start | bytes 1179656 | tf_op jit(solution)/shard_map/ppermute | solution.py:357
  89.7 42.0 %collective-permute-start.31 = (f32[384,512]{1,0:T(8,128)S(1)}, f32[384,512]{1,0:T(8,128)}, u32[]{:S(2)}, u32[]{:S(2)}) collective-permute-start(f32[384,512]{1,0:T(8,128)S(1)} %get-tuple-element.143.refs_2_), channel_id=1, source_target_pairs={{0,3},{1,2},{2,1},{3,0},{4,7},{5,6},{6,5},{7,4},{8,11},{9,10},{10,... | collective-permute-start | bytes 2359304 | tf_op jit(solution)/shard_map/ppermute | solution.py:364
  109.9 14.0 %collective-permute-start.21 = (f32[384,256]{1,0:T(8,128)}, f32[384,256]{1,0:T(8,128)S(1)}, u32[]{:S(2)}, u32[]{:S(2)}) collective-permute-start(f32[384,256]{1,0:T(8,128)} %collective-permute-done.17.refs_7_), channel_id=1, source_target_pairs={{0,8},{4,12},{8,16},{12,20},{16,24},{20,28},{24,0},{28,4},{1,9},{5... | collective-permute-start | bytes 1179656 | tf_op jit(solution)/shard_map/ppermute | solution.py:360
  110.0 21.7 %collective-permute-start.22 = (f32[384,256]{1,0:T(8,128)}, f32[384,256]{1,0:T(8,128)}, u32[]{:S(2)}, u32[]{:S(2)}) collective-permute-start(f32[384,256]{1,0:T(8,128)} %copy-done.23), channel_id=1, source_target_pairs={{0,8},{4,12},{8,16},{12,20},{16,24},{20,28},{24,0},{28,4},{1,9},{5... | collective-permute-start | bytes 1179656 | tf_op jit(solution)/shard_map/ppermute | solution.py:360
  110.1 21.6 %collective-permute-start.23 = (f32[384,256]{1,0:T(8,128)}, f32[384,256]{1,0:T(8,128)S(1)}, u32[]{:S(2)}, u32[]{:S(2)}) collective-permute-start(f32[384,256]{1,0:T(8,128)} %collective-permute-done.17.refs_7_), channel_id=1, source_target_pairs={{0,4},{4,0},{8,12},{12,8},{16,20},{20,16},{24,28},{28,24},{1,5},{5... | collective-permute-start | bytes 1179656 | tf_op jit(solution)/shard_map/ppermute | solution.py:357
  120.0 12.5 %collective-permute-start.24 = (f32[384,256]{1,0:T(8,128)}, f32[384,256]{1,0:T(8,128)S(1)}, u32[]{:S(2)}, u32[]{:S(2)}) collective-permute-start(f32[384,256]{1,0:T(8,128)} %copy-done.23), channel_id=1, source_target_pairs={{0,4},{4,0},{8,12},{12,8},{16,20},{20,16},{24,28},{28,24},{1,5},{5... | collective-permute-start | bytes 1179656 | tf_op jit(solution)/shard_map/ppermute | solution.py:357
  124.0 12.7 %copy-start.25 = (f32[384,256]{1,0:T(8,128)}, f32[384,256]{1,0:T(8,128)S(1)}, u32[]{:S(2)}) copy-start(f32[384,256]{1,0:T(8,128)S(1)} %collective-permute-done.21.refs_11_) | copy-start | bytes 1179652
  124.0 11.2 %collective-permute-start.27 = (f32[384,256]{1,0:T(8,128)S(1)}, f32[384,256]{1,0:T(8,128)S(1)}, u32[]{:S(2)}, u32[]{:S(2)}) collective-permute-start(f32[384,256]{1,0:T(8,128)S(1)} %collective-permute-done.21.refs_11_), channel_id=1, source_target_pairs={{0,4},{4,0},{8,12},{12,8},{16,20},{20,16},{24,28},{28,24},{1,5},{5... | collective-permute-start | bytes 1179656 | tf_op jit(solution)/shard_map/ppermute | solution.py:357
  131.7 4.3 %collective-permute-start.28 = (f32[384,256]{1,0:T(8,128)}, f32[384,256]{1,0:T(8,128)S(1)}, u32[]{:S(2)}, u32[]{:S(2)}) collective-permute-start(f32[384,256]{1,0:T(8,128)} %collective-permute-done.22.refs_12_), channel_id=1, source_target_pairs={{0,4},{4,0},{8,12},{12,8},{16,20},{20,16},{24,28},{28,24},{1,5},{5... | collective-permute-start | bytes 1179656 | tf_op jit(solution)/shard_map/ppermute | solution.py:357
  131.7 39.7 %collective-permute-start.14 = (f32[512,512]{1,0:T(8,128)}, f32[512,512]{1,0:T(8,128)}, u32[]{:S(2)}, u32[]{:S(2)}) collective-permute-start(f32[512,512]{1,0:T(8,128)} %get-tuple-element.93), channel_id=1, source_target_pairs={{0,1},{1,0},{2,3},{3,2},{4,5},{5,4},{6,7},{7,6},{8,9},{9,8},{10,11... | collective-permute-start | bytes 3145736 | tf_op jit(solution)/shard_map/ppermute | solution.py:417
  131.7 48.3 %collective-permute-start.15 = (f32[512,512]{1,0:T(8,128)}, f32[512,512]{1,0:T(8,128)S(1)}, u32[]{:S(2)}, u32[]{:S(2)}) collective-permute-start(f32[512,512]{1,0:T(8,128)} %get-tuple-element.94), channel_id=1, source_target_pairs={{0,2},{1,3},{2,0},{3,1},{4,6},{5,7},{6,4},{7,5},{8,10},{9,11},{10,... | collective-permute-start | bytes 3145736 | tf_op jit(solution)/shard_map/ppermute | solution.py:417
  132.5 47.5 %collective-permute-start.16 = (f32[512,512]{1,0:T(8,128)}, f32[512,512]{1,0:T(8,128)}, u32[]{:S(2)}, u32[]{:S(2)}) collective-permute-start(f32[512,512]{1,0:T(8,128)} %get-tuple-element.95), channel_id=1, source_target_pairs={{0,3},{1,2},{2,1},{3,0},{4,7},{5,6},{6,5},{7,4},{8,11},{9,10},{10,... | collective-permute-start | bytes 3145736 | tf_op jit(solution)/shard_map/ppermute | solution.py:417
  135.2 14.6 %collective-permute-start.25 = (f32[384,256]{1,0:T(8,128)S(1)}, f32[384,256]{1,0:T(8,128)S(1)}, u32[]{:S(2)}, u32[]{:S(2)}) collective-permute-start(f32[384,256]{1,0:T(8,128)S(1)} %collective-permute-done.21.refs_11_), channel_id=1, source_target_pairs={{0,8},{4,12},{8,16},{12,20},{16,24},{20,28},{24,0},{28,4},{1,9},{5... | collective-permute-start | bytes 1179656 | tf_op jit(solution)/shard_map/ppermute | solution.py:360
  136.7 19.6 %collective-permute-start.26 = (f32[384,256]{1,0:T(8,128)}, f32[384,256]{1,0:T(8,128)}, u32[]{:S(2)}, u32[]{:S(2)}) collective-permute-start(f32[384,256]{1,0:T(8,128)} %collective-permute-done.22.refs_12_), channel_id=1, source_target_pairs={{0,8},{4,12},{8,16},{12,20},{16,24},{20,28},{24,0},{28,4},{1,9},{5... | collective-permute-start | bytes 1179656 | tf_op jit(solution)/shard_map/ppermute | solution.py:360
  149.8 8.9 %copy-start.24 = (f32[384,256]{1,0:T(8,128)}, f32[384,256]{1,0:T(8,128)S(1)}, u32[]{:S(2)}) copy-start(f32[384,256]{1,0:T(8,128)S(1)} %collective-permute-done.25.refs_3_) | copy-start | bytes 1179652
  156.3 1.7 collective-permute-start.32
  156.3 2.4 collective-permute-start.33
  171.3 10.8 %copy-start.11 = (f32[512,512]{1,0:T(8,128)S(1)}, f32[512,512]{1,0:T(8,128)}, u32[]{:S(2)}) copy-start(f32[512,512]{1,0:T(8,128)} %get-tuple-element.138) | copy-start | bytes 3145732
  180.0 4.0 %copy-start.10 = (f32[512,512]{1,0:T(8,128)}, f32[512,512]{1,0:T(8,128)S(1)}, u32[]{:S(2)}) copy-start(f32[512,512]{1,0:T(8,128)S(1)} %collective-permute-done.15) | copy-start | bytes 3145732
  199.6 3.4 %collective-permute-start.41 = (f32[4,64,512]{2,1,0:T(8,128)}, f32[4,64,512]{2,1,0:T(8,128)S(1)}, u32[]{:S(2)}, u32[]{:S(2)}) collective-permute-start(f32[4,64,512]{2,1,0:T(8,128)} %get-tuple-element.153), channel_id=1, source_target_pairs={{0,4},{4,0},{8,12},{12,8},{16,20},{20,16},{24,28},{28,24},{1,5},{5... | collective-permute-start | bytes 1572872 | tf_op jit(solution)/shard_map/ppermute | solution.py:431
  200.8 4.8 %collective-permute-start.37 = (f32[4,64,512]{2,1,0:T(8,128)}, f32[4,64,512]{2,1,0:T(8,128)}, u32[]{:S(2)}, u32[]{:S(2)}) collective-permute-start(f32[4,64,512]{2,1,0:T(8,128)} %dynamic-slice_bitcast_fusion), channel_id=1, source_target_pairs={{0,4},{4,0},{8,12},{12,8},{16,20},{20,16},{24,28},{28,24},{1,5},{5... | collective-permute-start | bytes 1572872 | tf_op jit(solution)/shard_map/ppermute | solution.py:431
  201.0 45.3 %collective-permute-start.34 = (f32[384,512]{1,0:T(8,128)}, f32[384,512]{1,0:T(8,128)}, u32[]{:S(2)}, u32[]{:S(2)}) collective-permute-start(f32[384,512]{1,0:T(8,128)} %get-tuple-element.148.refs_7_), channel_id=1, source_target_pairs={{0,1},{1,0},{2,3},{3,2},{4,5},{5,4},{6,7},{7,6},{8,9},{9,8},{10,11... | collective-permute-start | bytes 2359304 | tf_op jit(solution)/shard_map/ppermute | solution.py:417
  202.7 43.7 %collective-permute-start.35 = (f32[384,512]{1,0:T(8,128)}, f32[384,512]{1,0:T(8,128)}, u32[]{:S(2)}, u32[]{:S(2)}) collective-permute-start(f32[384,512]{1,0:T(8,128)} %get-tuple-element.149.refs_8_), channel_id=1, source_target_pairs={{0,2},{1,3},{2,0},{3,1},{4,6},{5,7},{6,4},{7,5},{8,10},{9,11},{10,... | collective-permute-start | bytes 2359304 | tf_op jit(solution)/shard_map/ppermute | solution.py:417
  204.1 8.3 %collective-permute-start.42 = (f32[64,512]{1,0:T(8,128)S(1)}, f32[64,512]{1,0:T(8,128)S(1)}, u32[]{:S(2)}, u32[]{:S(2)}) collective-permute-start(f32[64,512]{1,0:T(8,128)S(1)} %get-tuple-element.162), channel_id=1, source_target_pairs={{0,8},{4,12},{8,16},{12,20},{16,24},{20,28},{24,0},{28,4},{1,9},{5... | collective-permute-start | bytes 393224 | tf_op jit(solution)/shard_map/ppermute | solution.py:435
  204.2 16.8 %collective-permute-start.43 = (f32[64,512]{1,0:T(8,128)S(1)}, f32[64,512]{1,0:T(8,128)S(1)}, u32[]{:S(2)}, u32[]{:S(2)}) collective-permute-start(f32[64,512]{1,0:T(8,128)S(1)} %get-tuple-element.164), channel_id=1, source_target_pairs={{0,16},{4,20},{8,24},{12,28},{16,0},{20,4},{24,8},{28,12},{1,17},{... | collective-permute-start | bytes 393224 | tf_op jit(solution)/shard_map/ppermute | solution.py:435
  205.6 15.4 %collective-permute-start.44 = (f32[64,512]{1,0:T(8,128)S(1)}, f32[64,512]{1,0:T(8,128)S(1)}, u32[]{:S(2)}, u32[]{:S(2)}) collective-permute-start(f32[64,512]{1,0:T(8,128)S(1)} %get-tuple-element.163), channel_id=1, source_target_pairs={{0,24},{4,28},{8,0},{12,4},{16,8},{20,12},{24,16},{28,20},{1,25},{... | collective-permute-start | bytes 393224 | tf_op jit(solution)/shard_map/ppermute | solution.py:435
  212.4 8.7 %collective-permute-start.38 = (f32[64,512]{1,0:T(8,128)S(1)}, f32[64,512]{1,0:T(8,128)S(1)}, u32[]{:S(2)}, u32[]{:S(2)}) collective-permute-start(f32[64,512]{1,0:T(8,128)S(1)} %get-tuple-element.165), channel_id=1, source_target_pairs={{0,8},{4,12},{8,16},{12,20},{16,24},{20,28},{24,0},{28,4},{1,9},{5... | collective-permute-start | bytes 393224 | tf_op jit(solution)/shard_map/ppermute | solution.py:435
  221.0 7.1 %collective-permute-start.39 = (f32[64,512]{1,0:T(8,128)S(1)}, f32[64,512]{1,0:T(8,128)S(1)}, u32[]{:S(2)}, u32[]{:S(2)}) collective-permute-start(f32[64,512]{1,0:T(8,128)S(1)} %get-tuple-element.167), channel_id=1, source_target_pairs={{0,16},{4,20},{8,24},{12,28},{16,0},{20,4},{24,8},{28,12},{1,17},{... | collective-permute-start | bytes 393224 | tf_op jit(solution)/shard_map/ppermute | solution.py:435
  221.0 25.3 %copy-start.3 = (f32[384,512]{1,0:T(8,128)S(1)}, f32[384,512]{1,0:T(8,128)}, u32[]{:S(2)}) copy-start(f32[384,512]{1,0:T(8,128)} %get-tuple-element.147.refs_6_) | copy-start | bytes 2359300
  221.0 8.7 %collective-permute-start.40 = (f32[64,512]{1,0:T(8,128)S(1)}, f32[64,512]{1,0:T(8,128)S(1)}, u32[]{:S(2)}, u32[]{:S(2)}) collective-permute-start(f32[64,512]{1,0:T(8,128)S(1)} %get-tuple-element.166), channel_id=1, source_target_pairs={{0,24},{4,28},{8,0},{12,4},{16,8},{20,12},{24,16},{28,20},{1,25},{... | collective-permute-start | bytes 393224 | tf_op jit(solution)/shard_map/ppermute | solution.py:435
  221.1 25.2 %collective-permute-start.36 = (f32[384,512]{1,0:T(8,128)}, f32[384,512]{1,0:T(8,128)S(1)}, u32[]{:S(2)}, u32[]{:S(2)}) collective-permute-start(f32[384,512]{1,0:T(8,128)} %get-tuple-element.150.refs_9_), channel_id=1, source_target_pairs={{0,3},{1,2},{2,1},{3,0},{4,7},{5,6},{6,5},{7,4},{8,11},{9,10},{10,... | collective-permute-start | bytes 2359304 | tf_op jit(solution)/shard_map/ppermute | solution.py:417
  230.2 10.3 %collective-permute-start.45 = (f32[2,64,128]{2,1,0:T(8,128)S(1)}, f32[2,64,128]{2,1,0:T(8,128)S(1)}, u32[]{:S(2)}, u32[]{:S(2)}) collective-permute-start(f32[2,64,128]{2,1,0:T(8,128)S(1)} %bitcast.98), channel_id=1, source_target_pairs={{0,1},{1,0},{2,3},{3,2},{4,5},{5,4},{6,7},{7,6},{8,9},{9,8},{10,11... | collective-permute-start | bytes 196616 | tf_op jit(solution)/shard_map/ppermute | solution.py:442
  231.7 10.2 %collective-permute-start.46 = (f32[2,64,128]{2,1,0:T(8,128)S(1)}, f32[2,64,128]{2,1,0:T(8,128)S(1)}, u32[]{:S(2)}, u32[]{:S(2)}) collective-permute-start(f32[2,64,128]{2,1,0:T(8,128)S(1)} %bitcast.97), channel_id=1, source_target_pairs={{0,2},{1,3},{2,0},{3,1},{4,6},{5,7},{6,4},{7,5},{8,10},{9,11},{10,... | collective-permute-start | bytes 196616 | tf_op jit(solution)/shard_map/ppermute | solution.py:442
  240.5 5.2 %collective-permute-start.47 = (f32[2,64,128]{2,1,0:T(8,128)S(1)}, f32[2,64,128]{2,1,0:T(8,128)S(1)}, u32[]{:S(2)}, u32[]{:S(2)}) collective-permute-start(f32[2,64,128]{2,1,0:T(8,128)S(1)} %bitcast.96), channel_id=1, source_target_pairs={{0,3},{1,2},{2,1},{3,0},{4,7},{5,6},{6,5},{7,4},{8,11},{9,10},{10,... | collective-permute-start | bytes 196616 | tf_op jit(solution)/shard_map/ppermute | solution.py:442
  (18 other events, 27.9 us)
